TPU v7x, 128 devices: a whole 4x4x4 slice. The times are simulated.
128 devices in a mesh: depth: 2 (over core), row: 2 (over x_hi), col: 32 (over z, y, x_lo).
Axes of the slice: x: 4 (x_hi: 2, x_lo: 2; x = x_hi * 2 + x_lo), y: 4, z: 4, core: 2. Of those that a mesh axis runs over, the one named last changes fastest.
Arguments:
- probe: float32 [2, 256, 256], replicated, may hold values from -6 to 6
- object_re: bfloat16 [2, 1024, 32768], P('depth', 'row', 'col'), may hold values from 0.099609375 to 1.8984375
- object_im: bfloat16 [2, 1024, 32768], P('depth', 'row', 'col'), may hold values from -1.796875 to 1.796875
- phases: float32 [256, 256], replicated, may hold values from -3.140625 to 3.140625
- centres: int32 [2, 32, 4, 2, 2], P('row', 'col'), may hold values from 0 to 1023, as said below
- occupied: int32 [2, 32, 4], P('row', 'col'), may hold values from 0 to 2, as said below
- measured: float32 [2, 32, 4, 2, 256, 256], P('row', 'col'), may hold values from 0 to 4
Outputs:
- object_grad: float32 [2, 2, 1024, 32768], P(None, 'depth', 'row', 'col')
- probe_grad: float32 [2, 256, 256], P(None, 'depth')
Inputs may be any that keep to these rules, and one draw needn't show every extreme that they name: `centres`: the 256 x 256 window around every centre, starting 256 // 2 pixels before it in both directions, lies inside the field of view. `occupied`: in every draw some tile has all 2 slots used in some micro-batch.
All inputs are finite; a program needn't handle non-finite values.
Results may differ from a plain program's by a relative error of at most 0.006.
Values may be sent and summed in bfloat16 or wider, within the bound.
A program may use at most 192 MiB of HBM per device.

v0:
```python
import math

import jax
import jax.numpy as jnp
from jax import lax
from jax.sharding import PartitionSpec as P

precise = lax.Precision.HIGH


def padded_2(array, sides, width):
    for axis, dim in sides:
        size, length = (lax.axis_size(axis), array.shape[dim])
        up = [(i, (i + 1) % size) for i in range(size - 1)]
        down = [(j, i) for i, j in up]
        last = lax.slice_in_dim(array, length - width, length, axis=dim)
        first = lax.slice_in_dim(array, 0, width, axis=dim)
        before = lax.ppermute(last, axis, up)
        after = lax.ppermute(first, axis, down)
        array = jnp.concatenate([before, array, after], axis=dim)
    return array


def as_sent(array):
    return jax.tree.map(lambda a: a.astype(jnp.bfloat16) if a.dtype == jnp.float32 else a, array)


def from_behind(block, axis, distance):
    devices = range(lax.axis_size(axis))
    route = [(i - distance, i) for i in devices if i - distance in devices]
    return lax.ppermute(block, axis, route)


def tables(frame_size):
    indices = jnp.arange(frame_size, dtype=jnp.int32)
    phase_turns = indices[:, None] * indices[None, :] % frame_size
    angles = phase_turns.astype(jnp.float32) * (-2.0 * math.pi / frame_size)
    scaling = 1.0 / math.sqrt(frame_size)
    return (jnp.cos(angles) * scaling, jnp.sin(angles) * scaling)


def complex_mul(left_re, left_im, right_re, right_im):
    return (left_re * right_re - left_im * right_im, left_re * right_im + left_im * right_re)


def conj_mul(left_re, left_im, right_re, right_im):
    return (left_re * right_re + left_im * right_im, left_re * right_im - left_im * right_re)


def apply_left(mat_re, mat_im, data_re, data_im):

    def product(matrix, data):
        return jnp.einsum("jk,bkl->bjl", matrix, data, precision=precise)

    return (
        product(mat_re, data_re) - product(mat_im, data_im),
        product(mat_re, data_im) + product(mat_im, data_re),
    )


def apply_right(data_re, data_im, mat_re, mat_im):

    def product(data, matrix):
        return jnp.einsum("bjk,kl->bjl", data, matrix, precision=precise)

    return (
        product(data_re, mat_re) - product(data_im, mat_im),
        product(data_re, mat_im) + product(data_im, mat_re),
    )


def transform(data_re, data_im, cosine, sines, direction):
    signed = sines * direction
    half_re, half_im = apply_left(cosine, signed, data_re, data_im)
    return apply_right(half_re, half_im, cosine, signed)


def shards(probe, object_re, object_im, phases, centres, occupied, measured):
    frame_size = probe.shape[1]
    half_size = frame_size // 2
    sections = lax.axis_size("depth")
    my_section = lax.axis_index("depth")
    tile_rows = object_re.shape[1]
    tile_cols = object_re.shape[2]
    batches = centres.shape[2]
    slot_count = centres.shape[3]
    cosine, sines = tables(frame_size)
    kern_re = jnp.cos(phases)
    kern_im = jnp.sin(phases)
    planes = jnp.stack([object_re[0], object_im[0]])
    padded = padded_2(planes, (("row", 1), ("col", 2)), half_size)
    groups = 1
    per_group = batches * slot_count // groups
    centre_px = centres[0, 0].reshape(groups, per_group, 2)
    slot_ids = jnp.arange(slot_count, dtype=jnp.int32)
    live_mask = (
        (slot_ids[None, :] < occupied[0, 0][:, None]).astype(jnp.float32).reshape(groups, per_group)
    )
    frames = measured[0, 0].reshape(groups, per_group, frame_size, frame_size)

    def window_at(centre):
        anchor = (jnp.zeros((), jnp.int32), centre[0], centre[1])
        return lax.dynamic_slice(padded, anchor, (2, frame_size, frame_size))

    windows = jax.vmap(jax.vmap(window_at, out_axes=1), out_axes=0)(centre_px).astype(jnp.float32)
    zero_wave = jnp.zeros((2, per_group, frame_size, frame_size), jnp.bfloat16)
    zero_field = jnp.zeros((2, per_group, frame_size, frame_size), jnp.float32)

    def propagate(data_re, data_im, direction):
        freq_re, freq_im = transform(data_re, data_im, cosine, sines, 1.0)
        kept_re, kept_im = complex_mul(freq_re, freq_im, kern_re, direction * kern_im)
        return transform(kept_re, kept_im, cosine, sines, -1.0)

    def carry_on(incoming, window, measure):
        exit_re, exit_im = complex_mul(incoming[0], incoming[1], window[0], window[1])
        out_re, out_im = propagate(exit_re, exit_im, 1.0)
        return (jnp.stack([out_re, out_im]).astype(jnp.bfloat16), zero_field)

    def detect(incoming, window, measure):
        exit_re, exit_im = complex_mul(incoming[0], incoming[1], window[0], window[1])
        freq_re, freq_im = transform(exit_re, exit_im, cosine, sines, 1.0)
        misfit = freq_re * freq_re + freq_im * freq_im - measure
        back_re, back_im = transform(misfit * freq_re, misfit * freq_im, cosine, sines, -1.0)
        return (zero_wave, jnp.stack([back_re, back_im]))

    def standby(incoming, window, measure):
        return (zero_wave, zero_field)

    launch = jnp.broadcast_to(probe[:, None], (2, per_group, frame_size, frame_size))
    steps_total = groups + sections - 1

    def forward_step(step_no, loop_state):
        received, inputs, farside = loop_state
        group_id = step_no - my_section
        active = (group_id >= 0) & (group_id < groups)
        group_at = jnp.clip(group_id, 0, groups - 1)
        target = jnp.where(active, group_at, groups)
        incoming = lax.cond(my_section == 0, lambda: launch, lambda: received.astype(jnp.float32))
        branch = jnp.where(active, jnp.where(my_section == sections - 1, 2, 1), 0)
        outgoing, far_adjoint = lax.switch(
            branch, [standby, carry_on, detect], incoming, windows[group_at], frames[group_at]
        )
        inputs = lax.dynamic_update_index_in_dim(inputs, incoming, target, 0)
        farside = lax.dynamic_update_index_in_dim(farside, far_adjoint, target, 0)
        received = jax.tree.map(
            lambda part, own: part.astype(own.dtype),
            from_behind(as_sent(outgoing), "depth", 1),
            outgoing,
        )
        return (received, inputs, farside)

    stored = jnp.zeros((groups + 1, 2, per_group, frame_size, frame_size), jnp.float32)
    _, inputs, farside = lax.fori_loop(0, steps_total, forward_step, (zero_wave, stored, stored))

    def hand_back(adjoint, window):
        pull_re, pull_im = conj_mul(window[0], window[1], adjoint[0], adjoint[1])
        out_re, out_im = propagate(pull_re, pull_im, -1.0)
        return (jnp.stack([out_re, out_im]).astype(jnp.bfloat16), jnp.stack([pull_re, pull_im]))

    def finish(adjoint, window):
        pull_re, pull_im = conj_mul(window[0], window[1], adjoint[0], adjoint[1])
        return (zero_wave, jnp.stack([pull_re, pull_im]))

    def pause(adjoint, window):
        return (zero_wave, zero_field)

    def backward_step(step_no, loop_state):
        received, gradient, probe_sum = loop_state
        group_id = step_no - (sections - 1 - my_section)
        active = (group_id >= 0) & (group_id < groups)
        group_at = jnp.clip(group_id, 0, groups - 1)
        adjoint = lax.cond(
            my_section == sections - 1,
            lambda: farside[group_at],
            lambda: received.astype(jnp.float32),
        )
        branch = jnp.where(active, jnp.where(my_section == 0, 2, 1), 0)
        outgoing, pulled = lax.switch(
            branch, [pause, hand_back, finish], adjoint, windows[group_at]
        )
        weight = live_mask[group_at] * active.astype(jnp.float32)
        incoming = inputs[group_at]
        grad_re, grad_im = conj_mul(incoming[0], incoming[1], adjoint[0], adjoint[1])
        update = jnp.stack([grad_re, grad_im]) * weight[None, :, None, None]
        places = centre_px[group_at]

        def deposit(slot_no, buffer):
            anchor = (jnp.zeros((), jnp.int32), places[slot_no, 0], places[slot_no, 1])
            current = lax.dynamic_slice(buffer, anchor, (2, frame_size, frame_size))
            addition = lax.dynamic_index_in_dim(update, slot_no, 1, False)
            return lax.dynamic_update_slice(buffer, current + addition, anchor)

        gradient = lax.fori_loop(0, per_group, deposit, gradient)
        anchor_flag = jnp.where(my_section == 0, 1.0, 0.0).astype(jnp.float32)
        probe_sum = probe_sum + jnp.sum(
            pulled * (weight * anchor_flag)[None, :, None, None], axis=1
        )
        received = jax.tree.map(
            lambda part, own: part.astype(own.dtype),
            from_behind(as_sent(outgoing), "depth", -1),
            outgoing,
        )
        return (received, gradient, probe_sum)

    gradient = jnp.zeros((2, tile_rows + 2 * half_size, tile_cols + 2 * half_size), jnp.float32)
    probe_sum = jnp.zeros((2, frame_size, frame_size), jnp.float32)
    _, gradient, probe_sum = lax.fori_loop(
        0, steps_total, backward_step, (zero_wave, gradient, probe_sum)
    )
    extended = padded_2(gradient.astype(jnp.bfloat16), (("row", 1), ("col", 2)), half_size).astype(
        gradient.dtype
    )
    rows_part = extended[:, 2 * half_size : 2 * half_size + tile_rows]
    rows_part = rows_part.at[:, :half_size].add(extended[:, :half_size])
    rows_part = rows_part.at[:, tile_rows - half_size :].add(
        extended[:, tile_rows + 3 * half_size :]
    )
    folded = rows_part[:, :, 2 * half_size : 2 * half_size + tile_cols]
    folded = folded.at[:, :, :half_size].add(rows_part[:, :, :half_size])
    folded = folded.at[:, :, tile_cols - half_size :].add(
        rows_part[:, :, tile_cols + 3 * half_size :]
    )
    tiles_summed = lax.psum(probe_sum, ("row", "col"))
    probe_share = lax.psum_scatter(
        tiles_summed.astype(jnp.bfloat16), "depth", scatter_dimension=1, tiled=True
    ).astype(jnp.float32)
    return (folded[:, None], probe_share)


def solution(mesh):
    in_specs = (
        P(),
        P("depth", "row", "col"),
        P("depth", "row", "col"),
        P(),
        P("row", "col", None, None, None),
        P("row", "col", None),
        P("row", "col", None, None, None, None),
    )
    out_specs = (P(None, "depth", "row", "col"), P(None, "depth", None))
    return jax.shard_map(shards, mesh=mesh, in_specs=in_specs, out_specs=out_specs, check_vma=False)
```

profile of v0, /device:TPU:0, one launch (start us, length us, event | category | flops | bytes accessed | tf_op | source)
XLA Modules:
  0.0 925.4 jit_solution(13366479959955847560)
XLA Ops:
  9.9 5.1 collective-permute-start.2
  16.4 9.9 %collective-permute-done.2 = bf16[2,128,1024]{2,1,0:T(8,128)(2,1)S(1)} collective-permute-done((bf16[2,128,1024]{2,1,0:T(8,128)(2,1)}, bf16[2,128,1024]{2,1,0:T(8,128)(2,1)S(1)}, u32[]{:S(2)}, u32[]{:S(2)}) %collective-permute-start.2) | collective-permute-done | bytes 524320 | tf_op jit(solution)/shard_map/ppermute | solution.py:18
  26.4 5.5 collective-permute-done.3
  43.0 11.3 %collective-permute-done.5 = bf16[2,768,128]{2,1,0:T(8,128)(2,1)} collective-permute-done((bf16[2,768,128]{2,1,0:T(8,128)(2,1)}, bf16[2,768,128]{2,1,0:T(8,128)(2,1)}, u32[]{:S(2)}, u32[]{:S(2)}) %collective-permute-start.5) | collective-permute-done | bytes 393248 | tf_op jit(solution)/shard_map/ppermute | solution.py:19
  57.6 31.1 %while.82 = (s32[]{:T(128)}, bf16[2,768,1280]{2,1,0:T(8,128)(2,1)}, s32[8,3]{0,1:T(4,128)S(1)}, bf16[8,2,256,256]{2,3,0,1:T(8,128)(2,1)}, s32[]{:T(128)}) while((s32[]{:T(128)}, bf16[2,768,1280]{2,1,0:T(8,128)(2,1)}, s32[8,3]{0,1:T(4,128)S(1)}, bf16[8,2,256,256]{2,3,0,1:T(8,128)(2,1)}, s32[]{:T(128)}) %tuple.288), condition=%wide.while_cond.4, body=%wide.while_body.4.sunk | while | flops 2 | bytes 1573489 | solution.py:103
  88.6 4.1 convert_bitcast_fusion
  92.7 4.3 broadcast_in_dim.90
  96.9 4.2 broadcast_in_dim.90.clone
  103.5 163.2 %while.83 = (s32[]{:T(128)}, bf16[2,8,256,256]{3,2,1,0:T(8,128)(2,1)}, f32[2,2,8,256,256]{4,3,2,1,0:T(8,128)}, f32[2,2,8,256,256]{4,3,2,1,0:T(8,128)}, s32[]{:T(...) while((s32[]{:T(128)}, ...), condition=%wide.region_6.7_spmd.clone.clone, body=%wide.region_0.6_spmd.clone.clone.sunk | while | flops 12907053056 | bytes 168297072 | solution.py:153
  109.3 62.9 %conditional.17 = (bf16[2,8,256,256]{3,2,1,0:T(8,128)(2,1)}, f32[1,2,8,256,256]{4,3,2,1,0:T(8,128)}) conditional(s32[]{:T(128)} %clamp.24, () %tuple.265, (f32[2,8,256,256]{3,2,1,0:T(8,128)}, f32[2,8,256,256]{2,3,1,0:T(8,128)}, f32[256,256]{1,0:T(8,128)S(1)}, f32[256,256]{1,0:T(8,128)S(1)}, f32[256,256]{1,0:T(8,128)S(1)}, ...), branch_computations={%region_3.3_spmd, %region_4.4_spmd, %region_5.5_spmd} | conditional | flops 12904038400 | bytes 136314896 | solution.py:140
  109.3 5.8 copy.139
  115.0 4.0 multiply_subtract_fusion.1
  130.8 12.3 %fusion.58 = f32[8,256,256]{2,1,0:T(8,128)S(1)} fusion(f32[8,256,256]{2,1,0:T(8,128)S(1)} %fusion.45, f32[8,256,256]{2,1,0:T(8,128)S(1)} %fusion.42, f32[256,256]{1,0:T(8,128)S(1)} %get-tuple-element.927, f32[256,256]{1,0:T(8,128)S(1)} %get-tuple-element.924, f32[256,256]{1,0:T(8,128)S(1)} %get-tuple-element.935), kind=kOutput, calls=%fused_computation.45 | convolution fusion | flops 806879232 | bytes 7077888 | tf_op jit(solution)/shard_map/while/body/eval_jaxpr/cond/branch_1_fun/jk,bkl->bjl/dot_general | solution.py:53
  174.8 7.6 bitcast_dynamic-update-slice_fusion.2
  188.1 4.2 conditional.17
  192.3 44.4 %collective-permute-start = (bf16[2,8,256,256]{3,2,1,0:T(8,128)(2,1)}, bf16[2,8,256,256]{3,2,1,0:T(8,128)(2,1)}, u32[]{:S(2)}, u32[]{:S(2)}) collective-permute-start(bf16[2,8,256,256]{3,2,1,0:T(8,128)(2,1)} %get-tuple-element.1823), channel_id=1, source_target_pairs={{0,64},{1,65},{2,66},{3,67},{4,68},{5,69},{6,70},{7,71},{8,72},{9,... | collective-permute-start | bytes 6291464 | tf_op jit(solution)/shard_map/while/body/eval_jaxpr/ppermute | solution.py:31
  236.7 7.5 bitcast_dynamic-update-slice_fusion.2
  271.9 254.9 %while.85 = (s32[]{:T(128)}, bf16[2,8,256,256]{3,2,1,0:T(8,128)(2,1)}, f32[2,768,1280]{2,1,0:T(8,128)}, f32[2,256,256]{1,2,0:T(8,128)}, s32[]{:T(128)}, /*index=...) while((s32[]{:T(128)}, ...), condition=%wide.region_16.17_spmd.clone.clone, body=%wide.region_7.16_spmd.clone.clone.sunk | while | flops 12911706112 | bytes 185599184 | solution.py:207
  272.0 4.0 conditional.18
  272.0 4.0 convert_element_type.43
  276.0 4.0 conditional.19
  284.4 4.2 multiply_add_fusion.12
  291.1 101.5 %while.86 = (s32[]{:T(128)}, f32[2,768,1280]{2,1,0:T(8,128)}, s32[8,2]{0,1:T(2,128)S(1)}, f32[2,8,256,256]{3,2,0,1:T(8,128)}, s32[]{:T(128)}, /*index=5*/s32[]{:T(128)}, s32[]{:T(128)}, s32[]{:T(128)}) while((s32[]{:T(128)}, f32[2,768,1280]{2,1,0:T(8,128)}, s32[8,2]{0,1:T(2,128)S(1)}, f32[2,8,256,256]{3,2,0,1:T(8,128)}, s32[]{:T(128)}, ...), condition=%wide.region_14.14_spmd, body=%wide.region_13.13_spmd.sunk | while | flops 131080 | bytes 2621629 | solution.py:193
  297.1 6.8 dynamic_update_slice.35
  309.9 6.5 dynamic_update_slice.35
  322.4 6.8 dynamic_update_slice.35
  335.2 6.7 dynamic_update_slice.35
  347.9 6.6 dynamic_update_slice.35
  360.5 6.8 dynamic_update_slice.35
  373.2 6.8 dynamic_update_slice.35
  386.0 6.6 dynamic_update_slice.35
  392.8 4.0 conditional.18
  396.8 13.4 %conditional.19 = (bf16[2,8,256,256]{3,2,1,0:T(8,128)(2,1)}, f32[2,8,256,256]{2,3,1,0:T(8,128)}) conditional(s32[]{:T(128)} %clamp.25, () %tuple.272, (f32[2,8,256,256]{2,3,1,0:T(8,128)}, f32[2,8,256,256]{3,2,1,0:T(8,128)}, f32[256,256]{1,0:T(8,128)S(1)}, f32[256,256]{1,0:T(8,128)S(1)}, f32[256,256]{1,0:T(8,128)S(1)}, ...), branch_computations={%region_10.10_spmd, %region_11.11_spmd.clone, %region_12.12_spmd} | conditional | flops 12902137856 | bytes 134217808 | solution.py:178
  396.8 5.4 copy.142
  402.2 4.1 multiply_add_fusion.5
  414.5 4.2 multiply_add_fusion.12
  421.3 101.5 %while.86 = (s32[]{:T(128)}, f32[2,768,1280]{2,1,0:T(8,128)}, s32[8,2]{0,1:T(2,128)S(1)}, f32[2,8,256,256]{3,2,0,1:T(8,128)}, s32[]{:T(128)}, /*index=5*/s32[]{:T(128)}, s32[]{:T(128)}, s32[]{:T(128)}) while((s32[]{:T(128)}, f32[2,768,1280]{2,1,0:T(8,128)}, s32[8,2]{0,1:T(2,128)S(1)}, f32[2,8,256,256]{3,2,0,1:T(8,128)}, s32[]{:T(128)}, ...), condition=%wide.region_14.14_spmd, body=%wide.region_13.13_spmd.sunk | while | flops 131080 | bytes 2621629 | solution.py:193
  427.3 6.8 dynamic_update_slice.35
  440.1 6.5 dynamic_update_slice.35
  452.5 6.8 dynamic_update_slice.35
  465.3 6.7 dynamic_update_slice.35
  478.0 6.6 dynamic_update_slice.35
  490.6 6.8 dynamic_update_slice.35
  503.4 6.8 dynamic_update_slice.35
  516.2 6.6 dynamic_update_slice.35
  537.0 355.4 %all-reduce.1 = bf16[2,256,256]{2,1,0:T(8,128)(2,1)} all-reduce(f32[2,256,256]{2,1,0:T(8,128)S(1)} %copy.150), channel_id=1, replica_groups=mesh['depth'=2,'row'=2,'col'=32] {'row','col'}, use_global_device_ids=true, to_apply=%region_17.18 | all-reduce | flops 131072 | bytes 786432 | tf_op jit(solution)/shard_map/psum | solution.py:223
  901.7 4.4 collective-permute-done.9
  906.1 6.3 maximum_convert_fusion
  (199 shorter events, 196.2 us)
Async XLA Ops:
  7.2 890.4 %reduce-scatter.2.cloned.1.call-start = ((), (), s32[]{:S(2)}) async-start(), calls=%async_computation.1 | async-start | bytes 393216 | tf_op jit(solution)/shard_map/reduce_scatter | solution.py:224
  7.2 1.5 copy-start.10
  8.8 7.5 copy-start.14
  9.9 16.5 %collective-permute-start.2 = (bf16[2,128,1024]{2,1,0:T(8,128)(2,1)}, bf16[2,128,1024]{2,1,0:T(8,128)(2,1)S(1)}, u32[]{:S(2)}, u32[]{:S(2)}) collective-permute-start(bf16[2,128,1024]{2,1,0:T(8,128)(2,1)} %get-tuple-element.1597), channel_id=1, source_target_pairs={{0,32},{1,33},{2,34},{3,35},{4,36},{5,37},{6,38},{7,39},{8,40},{9,... | collective-permute-start | bytes 1572872 | tf_op jit(solution)/shard_map/ppermute | solution.py:18
  14.9 17.0 %collective-permute-start.3 = (bf16[2,128,1024]{2,1,0:T(8,128)(2,1)}, bf16[2,128,1024]{2,1,0:T(8,128)(2,1)S(1)}, u32[]{:S(2)}, u32[]{:S(2)}) collective-permute-start(bf16[2,128,1024]{2,1,0:T(8,128)(2,1)} %get-tuple-element.1598), channel_id=1, source_target_pairs={{32,0},{33,1},{34,2},{35,3},{36,4},{37,5},{38,6},{39,7},{40,8},{41... | collective-permute-start | bytes 1572872 | tf_op jit(solution)/shard_map/ppermute | solution.py:19
  16.4 21.1 %copy-start.11 = (s32[1,8,2]{1,2,0:T(2,128)}, s32[1,8,2]{1,2,0:T(2,128)S(1)}, u32[]{:S(2)}) copy-start(s32[1,8,2]{1,2,0:T(2,128)S(1)} %reshape_squeeze.6) | copy-start | bytes 196
  31.9 5.7 copy-start.9
  33.0 10.0 %collective-permute-start.4 = (bf16[2,768,128]{2,1,0:T(8,128)(2,1)}, bf16[2,768,128]{2,1,0:T(8,128)(2,1)}, u32[]{:S(2)}, u32[]{:S(2)}) collective-permute-start(bf16[2,768,128]{2,1,0:T(8,128)(2,1)} %get-tuple-element.1595), channel_id=1, source_target_pairs={{0,1},{1,2},{2,3},{3,4},{4,5},{5,6},{6,7},{7,8},{8,9},{9,10},{10,1... | collective-permute-start | bytes 1179656 | tf_op jit(solution)/shard_map/ppermute | solution.py:18
  36.2 18.1 %collective-permute-start.5 = (bf16[2,768,128]{2,1,0:T(8,128)(2,1)}, bf16[2,768,128]{2,1,0:T(8,128)(2,1)}, u32[]{:S(2)}, u32[]{:S(2)}) collective-permute-start(bf16[2,768,128]{2,1,0:T(8,128)(2,1)} %get-tuple-element.1596), channel_id=1, source_target_pairs={{1,0},{2,1},{3,2},{4,3},{5,4},{6,5},{7,6},{8,7},{9,8},{10,9},{11,1... | collective-permute-start | bytes 1179656 | tf_op jit(solution)/shard_map/ppermute | solution.py:19
  101.2 2.3 copy-start
  172.1 10.3 %collective-permute-start = (bf16[2,8,256,256]{3,2,1,0:T(8,128)(2,1)}, bf16[2,8,256,256]{3,2,1,0:T(8,128)(2,1)}, u32[]{:S(2)}, u32[]{:S(2)}) collective-permute-start(bf16[2,8,256,256]{3,2,1,0:T(8,128)(2,1)} %get-tuple-element.1823), channel_id=1, source_target_pairs={{0,64},{1,65},{2,66},{3,67},{4,68},{5,69},{6,70},{7,71},{8,72},{9,... | collective-permute-start | bytes 6291464 | tf_op jit(solution)/shard_map/while/body/eval_jaxpr/ppermute | solution.py:31
  192.3 51.9 %collective-permute-start = (bf16[2,8,256,256]{3,2,1,0:T(8,128)(2,1)}, bf16[2,8,256,256]{3,2,1,0:T(8,128)(2,1)}, u32[]{:S(2)}, u32[]{:S(2)}) collective-permute-start(bf16[2,8,256,256]{3,2,1,0:T(8,128)(2,1)} %get-tuple-element.1823), channel_id=1, source_target_pairs={{0,64},{1,65},{2,66},{3,67},{4,68},{5,69},{6,70},{7,71},{8,72},{9,... | collective-permute-start | bytes 6291464 | tf_op jit(solution)/shard_map/while/body/eval_jaxpr/ppermute | solution.py:31
  270.4 1.5 copy-start.12
  270.4 1.5 copy-start.13
  280.1 112.6 %collective-permute-start.1 = (bf16[2,8,256,256]{3,2,1,0:T(8,128)(2,1)}, bf16[2,8,256,256]{3,2,1,0:T(8,128)(2,1)}, u32[]{:S(2)}, u32[]{:S(2)}) collective-permute-start(bf16[2,8,256,256]{3,2,1,0:T(8,128)(2,1)} %get-tuple-element.1842), channel_id=1, source_target_pairs={{64,0},{65,1},{66,2},{67,3},{68,4},{69,5},{70,6},{71,7},{72,8},{73... | collective-permute-start | bytes 6291464 | tf_op jit(solution)/shard_map/while/body/eval_jaxpr/ppermute | solution.py:31
  281.5 2.7 copy-start.5
  284.4 4.3 copy-start.6
  410.2 112.6 %collective-permute-start.1 = (bf16[2,8,256,256]{3,2,1,0:T(8,128)(2,1)}, bf16[2,8,256,256]{3,2,1,0:T(8,128)(2,1)}, u32[]{:S(2)}, u32[]{:S(2)}) collective-permute-start(bf16[2,8,256,256]{3,2,1,0:T(8,128)(2,1)} %get-tuple-element.1842), channel_id=1, source_target_pairs={{64,0},{65,1},{66,2},{67,3},{68,4},{69,5},{70,6},{71,7},{72,8},{73... | collective-permute-start | bytes 6291464 | tf_op jit(solution)/shard_map/while/body/eval_jaxpr/ppermute | solution.py:31
  411.7 2.7 copy-start.5
  414.5 4.3 copy-start.6
  530.4 1.9 copy-start.1
  532.4 4.5 copy-start.7
  533.3 359.1 %collective-permute-start.6 = (bf16[2,128,1280]{2,1,0:T(8,128)(2,1)}, bf16[2,128,1280]{2,1,0:T(8,128)(2,1)S(1)}, u32[]{:S(2)}, u32[]{:S(2)}) collective-permute-start(bf16[2,128,1280]{2,1,0:T(8,128)(2,1)} %get-tuple-element.1593), channel_id=1, source_target_pairs={{0,32},{1,33},{2,34},{3,35},{4,36},{5,37},{6,38},{7,39},{8,40},{9,... | collective-permute-start | bytes 1966088 | tf_op jit(solution)/shard_map/ppermute | solution.py:18
  535.5 356.9 %collective-permute-start.7 = (bf16[2,128,1280]{2,1,0:T(8,128)(2,1)S(1)}, bf16[2,128,1280]{2,1,0:T(8,128)(2,1)S(1)}, u32[]{:S(2)}, u32[]{:S(2)}) collective-permute-start(bf16[2,128,1280]{2,1,0:T(8,128)(2,1)S(1)} %get-tuple-element.1594), channel_id=1, source_target_pairs={{32,0},{33,1},{34,2},{35,3},{36,4},{37,5},{38,6},{39,7},{40,8},{41... | collective-permute-start | bytes 1966088 | tf_op jit(solution)/shard_map/ppermute | solution.py:19
  893.7 8.0 collective-permute-start.8
  895.0 11.1 %collective-permute-start.9 = (bf16[2,1024,128]{2,1,0:T(8,128)(2,1)S(1)}, bf16[2,1024,128]{2,1,0:T(8,128)(2,1)S(1)}, u32[]{:S(2)}, u32[]{:S(2)}) collective-permute-start(bf16[2,1024,128]{2,1,0:T(8,128)(2,1)S(1)} %get-tuple-element.1592), channel_id=1, source_target_pairs={{1,0},{2,1},{3,2},{4,3},{5,4},{6,5},{7,6},{8,7},{9,8},{10,9},{11,1... | collective-permute-start | bytes 1572872 | tf_op jit(solution)/shard_map/ppermute | solution.py:19
  912.4 2.1 copy-start.2
  916.4 2.0 copy-start.8
Sparse Core Ops, SparseCore 0:
  892.5 4.9 reduce-scatter.1
where the time goes:
time: 934 us; the launch traced here: 925 us
  blocking collectives  355 us (38%)
  local copies, waits for them, and re-layouts  223 us (24%)
  loops' own time  100 us (11%)
  other arithmetic  89.8 us (10%)
  starting transfers between devices  66.6 us (7%)
  waiting for transfers between devices  38.5 us (4%)
  matrix products  37.4 us (4%)
  between operations  14.5 us (2%)
    psum x1, blocking collectives, shards(): tiles_summed = lax.psum(probe_sum, ('row', 'col'))  355 us
    dynamic_update_slice x16, local copies, waits for them, and re-layouts, deposit(): return lax.dynamic_update_slice(buffer, current + addition, anchor)  107 us
    another operation x2, loops' own time, backward_step(): gradient = lax.fori_loop(0, per_group, deposit, gradient)  61.1 us
    ppermute x4, starting transfers between devices, from_behind(): return lax.ppermute(block, axis, route)  49.5 us
    gather x40, local copies, waits for them, and re-layouts  30.9 us
    add x16, other arithmetic, deposit(): return lax.dynamic_update_slice(buffer, current + addition, anchor)  24.4 us
    another operation x1, loops' own time, shards(): lax.fori_loop(0, steps_total, forward_step, (zero_wave, stored, stored))  23.1 us
    dot_general x8, matrix products, product(): return jnp.einsum('jk,bkl->bjl', matrix, data, precision=precise)  22.4 us
  transfers between devices with their start and end apart: 13, of which 7 were waited for; matrix products, arithmetic and copies ran while one was open for 20% of the time, Pallas kernels for 0%

commit v1 on v0

v1 whole, which is shorter than its diff:
```python
import functools

import jax
import jax.numpy as jnp
import numpy as np
from jax import lax
from jax.experimental import pallas as pl
from jax.experimental.pallas import tpu as pltpu
from jax.sharding import PartitionSpec as P

MESH = pl.DeviceIdType.MESH
F32 = jnp.float32
BF16 = jnp.bfloat16
ANY = pl.BlockSpec(memory_space=pl.ANY)
LANE = 128


def constants(n):
    half = n // 2
    k = np.arange(half)
    parts = []
    for parity in range(2):
        turns = (np.outer(2 * k + parity, k) % n) / n
        w = np.exp(-2j * np.pi * turns) / np.sqrt(n)
        block = np.block([[w.real, -w.imag], [w.imag, w.real]])
        for matrix in (block, block.T):
            high = matrix.astype(np.float32).astype(BF16)
            low = (matrix - high.astype(np.float64)).astype(np.float32).astype(BF16)
            parts += [high, low]
    order = np.concatenate([np.arange(0, n, 2), np.arange(1, n, 2)])
    perm = np.zeros((n, n), np.float32)
    perm[np.arange(n), order] = 1.0
    return np.stack(parts), np.stack([perm, perm.T]).astype(BF16)


def axis_ids():
    return lax.axis_index("depth"), lax.axis_index("row"), lax.axis_index("col")


def meet(peers):
    barrier = pltpu.get_barrier_semaphore()
    for peer in peers:
        pl.semaphore_signal(barrier, inc=1, device_id=peer, device_id_type=MESH)
    pl.semaphore_wait(barrier, len(peers))


def remote(src, dst, sems, slot, peer):
    return pltpu.make_async_remote_copy(
        src_ref=src, dst_ref=dst, send_sem=sems[0].at[slot], recv_sem=sems[1].at[slot], device_id=peer, device_id_type=MESH
    )


def neighbours():
    d, r, c = axis_ids()
    cols = lax.axis_size("col")
    right, left = lax.rem(c + 1, cols), lax.rem(c + cols - 1, cols)
    return [(d, 1 - r, c), (d, r, right), (d, r, left), (d, 1 - r, right), (d, 1 - r, left)]


def halo_kernel(rows, cols, halo, re_ref, im_ref, out_ref, stage, send, recv, own):
    _, r, _ = axis_ids()
    peers = neighbours()
    loads = [pltpu.make_async_copy(src.at[0], stage.at[p], own.at[p]) for p, src in enumerate((re_ref, im_ref))]
    for load in loads:
        load.start()
    meet(peers)
    edge = pl.ds(pl.multiple_of((rows - halo) * (1 - r), halo), halo)
    far = pl.ds(pl.multiple_of(rows * r, halo), halo)
    mine = pl.ds(pl.multiple_of(halo * r, halo), rows)
    everything, first, last = pl.ds(0, rows), pl.ds(0, halo), pl.ds(cols - halo, halo)
    middle, before, after = pl.ds(halo, cols), pl.ds(0, halo), pl.ds(halo + cols, halo)
    moves = [
        (edge, pl.ds(0, cols), far, middle),
        (everything, last, mine, before),
        (everything, first, mine, after),
        (edge, last, far, before),
        (edge, first, far, after),
    ]
    copies = []
    for p, src in enumerate((re_ref, im_ref)):
        for i, (sr, sc, dr, dc) in enumerate(moves):
            copies.append(remote(src.at[0, sr, sc], out_ref.at[p, dr, dc], (send, recv), p * 5 + i, peers[i]))
    for copy in copies:
        copy.start()
    stores = [pltpu.make_async_copy(stage.at[p], out_ref.at[p, mine, middle], own.at[2 + p]) for p in range(2)]
    for load, store in zip(loads, stores):
        load.wait()
        store.start()
    for store in stores:
        store.wait()
    for copy in copies:
        copy.wait()


def exchange_halo(object_re, object_im, halo):
    _, rows, cols = object_re.shape
    return pl.pallas_call(
        functools.partial(halo_kernel, rows, cols, halo),
        out_shape=jax.ShapeDtypeStruct((2, rows + halo, cols + 2 * halo), object_re.dtype),
        in_specs=[ANY, ANY],
        out_specs=ANY,
        scratch_shapes=[
            pltpu.VMEM((2, rows, cols), object_re.dtype),
            pltpu.SemaphoreType.DMA((10,)),
            pltpu.SemaphoreType.DMA((10,)),
            pltpu.SemaphoreType.DMA((4,)),
        ],
        compiler_params=pltpu.CompilerParams(collective_id=0, has_side_effects=True),
        name="halo_in",
    )(object_re, object_im)


def shifted_in(x, down, right):
    rows, cols = x.shape
    turned = pltpu.roll(x.reshape(rows // 8, 8, cols), jnp.bitwise_and(8 - down, 7), 1)
    sub = lax.broadcasted_iota(jnp.int32, (rows // 8 - 1, 8, cols), 1)
    x = jnp.where(sub < 8 - down, turned[:-1], turned[1:]).reshape(rows - 8, cols)
    turned = [pltpu.roll(x[:, i : i + LANE], jnp.bitwise_and(LANE - right, LANE - 1), 1) for i in range(0, cols, LANE)]
    lanes = lax.broadcasted_iota(jnp.int32, turned[0].shape, 1)
    return jnp.concatenate([jnp.where(lanes < LANE - right, a, b) for a, b in zip(turned[:-1], turned[1:])], 1)


def shifted_out(x, down, right):
    rows, cols = x.shape
    turned = [pltpu.roll(x[:, i : i + LANE], right, 1) for i in range(0, cols, LANE)]
    lanes = lax.broadcasted_iota(jnp.int32, turned[0].shape, 1)
    none = jnp.zeros_like(turned[0])
    x = jnp.concatenate([jnp.where(lanes < right, a, b) for a, b in zip([none] + turned, turned + [none])], 1)
    cols = cols + LANE
    turned = pltpu.roll(x.reshape(rows // 8, 8, cols), down, 1)
    none = jnp.zeros((1, 8, cols), x.dtype)
    sub = lax.broadcasted_iota(jnp.int32, (rows // 8 + 1, 8, cols), 1)
    both = jnp.where(sub < down, jnp.concatenate([none, turned], 0), jnp.concatenate([turned, none], 0))
    return both.reshape(rows + 8, cols)


def extract_kernel(n, rows_all, at_ref, pad_ref, mine_ref, theirs_ref, wide):
    k = pl.program_id(0)
    row, col = at_ref[k, 0], at_ref[k, 1]
    tall = n + 16
    base = pl.multiple_of(jnp.minimum(row // 16 * 16, rows_all - tall), 16)
    lane = pl.multiple_of(col // LANE * LANE, LANE)
    down, right = row - base, col - lane
    skip = pl.multiple_of(down // 8 * 8, 8)
    down = down - skip
    for p in range(2):
        wide[pl.ds(0, tall), :] = pad_ref[p, pl.ds(base, tall), pl.ds(lane, n + LANE)].astype(F32)
        window = shifted_in(wide[pl.ds(skip, n + 8), :], down, right).astype(BF16)
        @pl.when(k < 4)
        def _():
            mine_ref[0, p] = window
        @pl.when(k >= 4)
        def _():
            theirs_ref[0, p] = window


def extract(starts, padded, n):
    count = starts.shape[0]
    half = count // 2
    rows_all, cols_all = padded.shape[1:]
    shape = jax.ShapeDtypeStruct((half, 2, n, n), BF16)
    return pl.pallas_call(
        functools.partial(extract_kernel, n, rows_all),
        out_shape=(shape, shape),
        grid_spec=pltpu.PrefetchScalarGridSpec(
            num_scalar_prefetch=1,
            grid=(count,),
            in_specs=[pl.BlockSpec((2, rows_all, cols_all), lambda k, at: (0, 0, 0), pipeline_mode=pl.Buffered(1))],
            out_specs=(
                pl.BlockSpec((1, 2, n, n), lambda k, at: (jnp.minimum(k, half - 1), 0, 0, 0)),
                pl.BlockSpec((1, 2, n, n), lambda k, at: (jnp.maximum(k - half, 0), 0, 0, 0)),
            ),
            scratch_shapes=[pltpu.VMEM((n + 24, n + LANE), F32)],
        ),
        name="extract",
    )(starts, padded)


def swap_kernel(count, *refs):
    d, r, c = axis_ids()
    peer = (1 - d, r, c)
    sources, targets, (send, recv) = refs[:count], refs[count : 2 * count], refs[2 * count :]
    meet([peer])
    copies = [remote(s, t, (send, recv), i, peer) for i, (s, t) in enumerate(zip(sources, targets))]
    for copy in copies:
        copy.start()
    for copy in copies:
        copy.wait()


def swap(arrays, collective_id, name):
    count = len(arrays)
    return pl.pallas_call(
        functools.partial(swap_kernel, count),
        out_shape=tuple(jax.ShapeDtypeStruct(a.shape, a.dtype) for a in arrays),
        in_specs=[ANY] * count,
        out_specs=tuple([ANY] * count),
        scratch_shapes=[pltpu.SemaphoreType.DMA((count,)), pltpu.SemaphoreType.DMA((count,))],
        compiler_params=pltpu.CompilerParams(collective_id=collective_id, has_side_effects=True),
        name=name,
    )(*arrays)


def split(x):
    high = x.astype(BF16)
    return high, (x - high.astype(F32)).astype(BF16)


def product(a, b, passes):
    (ah, al), (bh, bl) = a, b
    if passes == 3:
        lhs, rhs = [ah, ah, al], [bh, bl, bh]
    else:
        lhs, rhs = [ah], [bh]
    lhs = jnp.concatenate(lhs, 1) if len(lhs) > 1 else lhs[0]
    rhs = jnp.concatenate(rhs, 0) if len(rhs) > 1 else rhs[0]
    return jnp.dot(lhs, rhs, preferred_element_type=F32)


def make_transforms(mats_ref):
    def mat(parity, transposed):
        at = parity * 4 + transposed * 2
        return mats_ref[at], mats_ref[at + 1]

    def forward(zr, zi):
        h = zr.shape[0] // 2
        outs = []
        for parity in range(2):
            fold = (lambda z: z[:h] + z[h:]) if parity == 0 else (lambda z: z[:h] - z[h:])
            outs.append(product(mat(parity, 0), split(jnp.concatenate([fold(zr), fold(zi)], 0)), 3))
        yr = jnp.concatenate([outs[0][:h], outs[1][:h]], 0)
        yi = jnp.concatenate([outs[0][h:], outs[1][h:]], 0)
        outs = []
        for parity in range(2):
            fold = (lambda z: z[:, :h] + z[:, h:]) if parity == 0 else (lambda z: z[:, :h] - z[:, h:])
            outs.append(product(split(jnp.concatenate([fold(yr), fold(yi)], 1)), mat(parity, 1), 3))
        return (
            jnp.concatenate([outs[0][:, :h], outs[1][:, :h]], 1),
            jnp.concatenate([outs[0][:, h:], outs[1][:, h:]], 1),
        )

    def inverse(zr, zi):
        h = zr.shape[0] // 2
        e = product(mat(0, 1), split(jnp.concatenate([zr[:h], zi[:h]], 0)), 3)
        o = product(mat(1, 1), split(jnp.concatenate([zr[h:], zi[h:]], 0)), 3)
        yr = jnp.concatenate([e[:h] + o[:h], e[:h] - o[:h]], 0)
        yi = jnp.concatenate([e[h:] + o[h:], e[h:] - o[h:]], 0)
        e = product(split(jnp.concatenate([yr[:, :h], yi[:, :h]], 1)), mat(0, 0), 3)
        o = product(split(jnp.concatenate([yr[:, h:], yi[:, h:]], 1)), mat(1, 0), 3)
        return (
            jnp.concatenate([e[:, :h] + o[:, :h], e[:, :h] - o[:, :h]], 1),
            jnp.concatenate([e[:, h:] + o[:, h:], e[:, h:] - o[:, h:]], 1),
        )

    return forward, inverse


def cmul(ar, ai, br, bi):
    return ar * br - ai * bi, ar * bi + ai * br


def conj_mul(ar, ai, br, bi):
    return ar * br + ai * bi, ar * bi - ai * br


def rounded(x):
    return x.astype(BF16).astype(F32)


def wave_kernel(half, info_ref, probe_ref, phases_ref, mats_ref, perm_ref, mine_ref, other_ref, frame_ref, grads_ref, keep_ref, give_ref, kern, total):
    k = pl.program_id(0)
    d = info_ref[0]
    forward, inverse = make_transforms(mats_ref)

    def reorder(x, rows):
        high, low = split(x)
        if rows:
            high = jnp.dot(perm_ref[0], high, preferred_element_type=F32).astype(BF16)
            low = jnp.dot(perm_ref[0], low, preferred_element_type=F32).astype(BF16)
        return jnp.dot(high, perm_ref[1], preferred_element_type=F32) + jnp.dot(low, perm_ref[1], preferred_element_type=F32)

    @pl.when(k == 0)
    def _():
        kern[0] = reorder(jnp.cos(phases_ref[...]), True)
        kern[1] = reorder(jnp.sin(phases_ref[...]), True)
        total[...] = jnp.zeros_like(total)

    live = info_ref[1 + k].astype(F32)
    first = d == 0

    def window(s):
        pick = first if s == 0 else jnp.logical_not(first)
        return [jnp.where(pick, mine_ref[0, p], other_ref[0, p]).astype(F32) for p in range(2)]

    w0r, w0i = window(0)
    fr, fi = forward(*cmul(probe_ref[0], probe_ref[1], w0r, w0i))
    pr, pi = inverse(*cmul(fr, fi, kern[0], kern[1]))
    pr, pi = rounded(pr), rounded(pi)
    w1r, w1i = window(1)
    fr, fi = forward(*cmul(pr, pi, w1r, w1i))
    misfit = fr * fr + fi * fi - reorder(frame_ref[0], True)
    xr, xi = inverse(misfit * fr, misfit * fi)
    gr, gi = conj_mul(pr, pi, xr, xi)
    grads_ref[1, 0, 0] = (gr * live).astype(BF16)
    grads_ref[1, 0, 1] = (gi * live).astype(BF16)
    fr, fi = forward(*conj_mul(w1r, w1i, xr, xi))
    xr, xi = inverse(*conj_mul(kern[0], kern[1], fr, fi))
    xr, xi = rounded(xr), rounded(xi)
    gr, gi = conj_mul(probe_ref[0], probe_ref[1], xr, xi)
    grads_ref[0, 0, 0] = (gr * live).astype(BF16)
    grads_ref[0, 0, 1] = (gi * live).astype(BF16)
    w0r, w0i = window(0)
    lr, li = conj_mul(w0r, w0i, xr, xi)
    total[0] += lr * live
    total[1] += li * live

    @pl.when(k == half - 1)
    def _():
        n = total.shape[1]
        h = n // 2
        for p in range(2):
            keep_ref[p] = jnp.where(first, total[p, :h], total[p, h:])
            give_ref[p] = jnp.where(first, total[p, h:], total[p, :h]).astype(BF16)


def waves(info, probe, phases, mine, other, frames):
    half, _, n, _ = mine.shape
    mats, perm = constants(n)
    fixed = lambda shape: pl.BlockSpec(shape, lambda k, i: (0,) * len(shape), pipeline_mode=pl.Buffered(1))
    window = pl.BlockSpec((1, 2, n, n), lambda k, i: (k, 0, 0, 0))
    return pl.pallas_call(
        functools.partial(wave_kernel, half),
        out_shape=(
            jax.ShapeDtypeStruct((2, half, 2, n, n), BF16),
            jax.ShapeDtypeStruct((2, n // 2, n), F32),
            jax.ShapeDtypeStruct((2, n // 2, n), BF16),
        ),
        grid_spec=pltpu.PrefetchScalarGridSpec(
            num_scalar_prefetch=1,
            grid=(half,),
            in_specs=[
                fixed((2, n, n)),
                fixed((n, n)),
                fixed(mats.shape),
                fixed(perm.shape),
                window,
                window,
                pl.BlockSpec((1, n, n), lambda k, i: (i[0] * half + k, 0, 0)),
            ],
            out_specs=(
                pl.BlockSpec((2, 1, 2, n, n), lambda k, i: (0, k, 0, 0, 0)),
                pl.BlockSpec((2, n // 2, n), lambda k, i: (0, 0, 0)),
                pl.BlockSpec((2, n // 2, n), lambda k, i: (0, 0, 0)),
            ),
            scratch_shapes=[pltpu.VMEM((2, n, n), F32), pltpu.VMEM((2, n, n), F32)],
        ),
        name="waves",
    )(info, probe, phases, jnp.asarray(mats), jnp.asarray(perm), mine, other, frames)


def scatter_kernel(half, rows, cols, halo, at_ref, mine_ref, got_ref, centre_ref, row_ref, side_ref, corner_ref, acc):
    k = pl.program_id(0)
    n = mine_ref.shape[-1]

    @pl.when(k == 0)
    def _():
        acc[...] = jnp.zeros_like(acc)

    row, col = at_ref[k, 0], at_ref[k, 1]
    lane = pl.multiple_of(col // LANE * LANE, LANE)
    top = pl.multiple_of(row // 8 * 8, 8)
    for p in range(2):
        x = jnp.where(k < half, mine_ref[0, 0, p], got_ref[0, p]).astype(F32)
        acc[p, pl.ds(top, n + 8), pl.ds(lane, n + LANE)] += shifted_out(x, row - top, col - lane)

    @pl.when(k == 2 * half - 1)
    def _():
        up = at_ref[2 * half, 0]
        mine = pl.ds(pl.multiple_of(halo * up, halo), rows)
        far = pl.ds(pl.multiple_of(rows * (1 - up), halo), halo)
        for p in range(2):
            centre_ref[p] = acc[p, mine, pl.ds(halo, cols)]
            row_ref[p] = acc[p, far, pl.ds(halo, cols)].astype(BF16)
            for i, at in enumerate((halo + cols, 0)):
                side_ref[i, p] = acc[p, mine, pl.ds(at, halo)].astype(BF16)
                corner_ref[i, p] = acc[p, far, pl.ds(at, halo)].astype(BF16)


def scatter(places, grads, got, rows, cols, halo):
    half, _, n, _ = got.shape
    full = lambda shape: pl.BlockSpec(shape, lambda k, i: (0,) * len(shape))
    shapes = [((2, rows, cols), F32), ((2, halo, cols), BF16), ((2, 2, rows, halo), BF16), ((2, 2, halo, halo), BF16)]
    return pl.pallas_call(
        functools.partial(scatter_kernel, half, rows, cols, halo),
        out_shape=tuple(jax.ShapeDtypeStruct(s, t) for s, t in shapes),
        grid_spec=pltpu.PrefetchScalarGridSpec(
            num_scalar_prefetch=1,
            grid=(2 * half,),
            in_specs=[
                pl.BlockSpec((1, 1, 2, n, n), lambda k, i: (i[2 * half, 1], jnp.minimum(k, half - 1), 0, 0, 0)),
                pl.BlockSpec((1, 2, n, n), lambda k, i: (jnp.maximum(k - half, 0), 0, 0, 0)),
            ],
            out_specs=tuple(full(s) for s, _ in shapes),
            scratch_shapes=[pltpu.VMEM((2, rows + halo + 8, cols + 2 * halo), F32)],
        ),
        name="scatter",
    )(places, grads, got)


def x_peer(q):
    d, _, c = axis_ids()
    return (d, q // 2, c // 2 * 2 + lax.rem(q, 2))


def plane_peer(q):
    d, r, c = axis_ids()
    return (d, r, q * 2 + lax.rem(c, 2))


def return_kernel(row_ref, side_ref, corner_ref, keep_ref, got_ref, row_out, side_out, corner_out, probe_out, buf, line, plane, gathered, strips, xs, ps, gs, fs):
    d, r, c = axis_ids()
    planes = lax.axis_size("col") // 2
    my_x = r * 2 + lax.rem(c, 2)
    my_p = c // 2
    peers = neighbours()
    line_peers = [lax.rem(my_x + t, 4) for t in range(1, 4)]
    plane_peers = [lax.rem(my_p + t, planes) for t in range(1, planes)]
    meet(peers + [x_peer(q) for q in line_peers] + [plane_peer(q) for q in plane_peers])
    pairs = [
        (row_ref, row_out, peers[0]),
        (side_ref.at[0], side_out.at[0], peers[1]),
        (side_ref.at[1], side_out.at[1], peers[2]),
        (corner_ref.at[0], corner_out.at[0], peers[3]),
        (corner_ref.at[1], corner_out.at[1], peers[4]),
    ]
    copies = [remote(s, t, strips, i, peer) for i, (s, t, peer) in enumerate(pairs)]
    for copy in copies:
        copy.start()
    half_rows, n = keep_ref.shape[1:]
    at = 0
    for p in range(2):
        for t in range(half_rows // 8):
            for h in range(n // LANE):
                place = (p, pl.ds(8 * t, 8), pl.ds(LANE * h, LANE))
                buf[at] = keep_ref[place] + got_ref[place].astype(F32)
                at += 1
    share = at // 4

    def piece(ref, q):
        return ref.at[pl.ds(q * share, share)]

    sent = []
    for q in line_peers:
        sent.append(pltpu.make_async_remote_copy(piece(buf, q), line.at[my_x], xs[0].at[q], xs[1].at[my_x], device_id=x_peer(q), device_id_type=MESH))
        sent[-1].start()
    for q in line_peers:
        pltpu.make_async_remote_copy(piece(buf, q), line.at[q], xs[0].at[q], xs[1].at[q], device_id=x_peer(q), device_id_type=MESH).wait_recv()
    total = buf[pl.ds(my_x * share, share)]
    for q in line_peers:
        total = total + line[q]
    plane[my_p] = total
    for q in plane_peers:
        sent.append(pltpu.make_async_remote_copy(plane.at[my_p, q], gathered.at[my_p], ps[0].at[q], ps[1].at[my_p], device_id=plane_peer(q), device_id_type=MESH))
        sent[-1].start()
    for q in plane_peers:
        pltpu.make_async_remote_copy(plane.at[my_p, q], gathered.at[q], ps[0].at[q], ps[1].at[q], device_id=plane_peer(q), device_id_type=MESH).wait_recv()
    mine = plane[my_p, my_p]
    for q in plane_peers:
        mine = mine + gathered[q]
    probe_out[my_x * share + my_p] = mine
    own = probe_out.at[my_x * share + my_p]
    for q in plane_peers:
        sent.append(pltpu.make_async_remote_copy(own, own, gs[0].at[q], gs[1].at[my_p], device_id=plane_peer(q), device_id_type=MESH))
        sent[-1].start()
    for q in plane_peers:
        there = probe_out.at[my_x * share + q]
        pltpu.make_async_remote_copy(there, there, gs[0].at[q], gs[1].at[q], device_id=plane_peer(q), device_id_type=MESH).wait_recv()
    for q in line_peers:
        block = piece(probe_out, my_x)
        sent.append(pltpu.make_async_remote_copy(block, block, fs[0].at[q], fs[1].at[my_x], device_id=x_peer(q), device_id_type=MESH))
        sent[-1].start()
    for q in line_peers:
        block = piece(probe_out, q)
        pltpu.make_async_remote_copy(block, block, fs[0].at[q], fs[1].at[q], device_id=x_peer(q), device_id_type=MESH).wait_recv()
    for copy in sent:
        copy.wait_send()
    for copy in copies:
        copy.wait()


def send_back(row, side, corner, keep, got):
    chunks = keep.size // (8 * LANE)
    share = chunks // 4
    vmem = pl.BlockSpec(memory_space=pltpu.VMEM)
    dma = lambda n: [pltpu.SemaphoreType.DMA((n,)), pltpu.SemaphoreType.DMA((n,))]
    return pl.pallas_call(
        return_kernel_flat,
        out_shape=tuple(jax.ShapeDtypeStruct(a.shape, a.dtype) for a in (row, side, corner)) + (jax.ShapeDtypeStruct((chunks, 8, LANE), F32),),
        in_specs=[ANY, ANY, ANY, vmem, vmem],
        out_specs=(ANY, ANY, ANY, vmem),
        scratch_shapes=[
            pltpu.VMEM((chunks, 8, LANE), F32),
            pltpu.VMEM((4, share, 8, LANE), F32),
            pltpu.VMEM((share, share, 8, LANE), F32),
            pltpu.VMEM((share, 8, LANE), F32),
        ]
        + dma(5) + dma(4) + dma(share) + dma(share) + dma(4),
        compiler_params=pltpu.CompilerParams(collective_id=3, has_side_effects=True),
        name="halo_out",
    )(row, side, corner, keep, got)


def return_kernel_flat(*refs):
    sems = refs[13:]
    return_kernel(*refs[:13], *[sems[i : i + 2] for i in range(0, 10, 2)])


def fold_kernel(halo, info_ref, centre_ref, row_ref, side_ref, corner_ref, chunks_ref, out_ref, probe_ref):
    up = info_ref[0]
    _, rows, cols = centre_ref.shape
    edge = pl.ds(pl.multiple_of((rows - halo) * (1 - up), halo), halo)
    out_ref[:, 0] = centre_ref[...]
    for p in range(2):
        out_ref[p, 0, edge, :] += row_ref[p].astype(F32)
        for i, at in enumerate((0, cols - halo)):
            lanes = pl.ds(at, halo)
            out_ref[p, 0, :, lanes] += side_ref[i, p].astype(F32)
            out_ref[p, 0, edge, lanes] += corner_ref[i, p].astype(F32)
    at = 0
    _, half_rows, n = probe_ref.shape
    for p in range(2):
        for t in range(half_rows // 8):
            for h in range(n // LANE):
                probe_ref[p, pl.ds(8 * t, 8), pl.ds(LANE * h, LANE)] = chunks_ref[at]
                at += 1


def fold(info, centre, row, side, corner, chunks, n):
    halo = row.shape[1]
    _, rows, cols = centre.shape
    return pl.pallas_call(
        functools.partial(fold_kernel, halo),
        out_shape=(jax.ShapeDtypeStruct((2, 1, rows, cols), F32), jax.ShapeDtypeStruct((2, n // 2, n), F32)),
        in_specs=[pl.BlockSpec(memory_space=pltpu.SMEM)] + [pl.BlockSpec(memory_space=pltpu.VMEM)] * 5,
        out_specs=(pl.BlockSpec(memory_space=pltpu.VMEM),) * 2,
        name="fold",
    )(info, centre, row, side, corner, chunks)


def shards(probe, object_re, object_im, phases, centres, occupied, measured):
    n = probe.shape[1]
    halo = n // 2
    _, rows, cols = object_re.shape
    batches, slots = centres.shape[2:4]
    count = batches * slots
    half = count // 2
    d, r, _ = axis_ids()
    starts = centres[0, 0].reshape(count, 2) + jnp.stack([halo * (r - 1), jnp.zeros_like(r)])
    starts = jnp.where(d == 0, starts, jnp.concatenate([starts[half:], starts[:half]]))
    live = (jnp.arange(slots, dtype=jnp.int32)[None] < occupied[0, 0][:, None]).reshape(2, half).astype(jnp.int32)
    info = jnp.concatenate([d[None].astype(jnp.int32), jnp.where(d == 0, live[0], live[1])])
    places = jnp.concatenate([starts, jnp.stack([r, d])[None].astype(jnp.int32)])
    padded = exchange_halo(object_re, object_im, halo)
    mine, theirs = extract(starts, padded, n)
    (other,) = swap((theirs,), 1, "swap_in")
    grads, keep, give = waves(info, probe, phases, mine, other, measured[0, 0].reshape(count, n, n))
    away = lax.dynamic_index_in_dim(grads, 1 - d, 0, False)
    got, given = swap((away, give), 2, "swap_out")
    centre, row, side, corner = scatter(places, grads, got, rows, cols, halo)
    row, side, corner, chunks = send_back(row, side, corner, keep, given)
    return fold(r[None].astype(jnp.int32), centre, row, side, corner, chunks, n)


def solution(mesh):
    in_specs = (
        P(),
        P("depth", "row", "col"),
        P("depth", "row", "col"),
        P(),
        P("row", "col", None, None, None),
        P("row", "col", None),
        P("row", "col", None, None, None, None),
    )
    out_specs = (P(None, "depth", "row", "col"), P(None, "depth", None))
    return jax.shard_map(shards, mesh=mesh, in_specs=in_specs, out_specs=out_specs, check_vma=False)
```

time: 934 us -> 144 us (0.15)
  blocking collectives: 355 us -> 0 us
  local copies, waits for them, and re-layouts: 223 us -> 3.88 us
  Pallas kernels: 0 us -> 136 us
  loops' own time: 100 us -> 0 us
  other arithmetic: 89.8 us -> 2.75 us
  starting transfers between devices: 66.6 us -> 0 us
  waiting for transfers between devices: 38.5 us -> 0 us
  matrix products: 37.4 us -> 0 us
  between operations: 14.5 us -> 0.7 us
    psum x1 -> x0, blocking collectives: 355 us -> none  [shards(): tiles_summed = lax.psum(probe_sum, ('row', 'col'))]
    pallas_call x0 -> x8, Pallas kernels: none -> 136 us  [the longest x1 51.6 us: send_back(): pl.pallas_call(return_kernel_flat, out_shape=tuple((jax.ShapeDtypeStruct(...]
    dynamic_update_slice x18 -> x0, local copies, waits for them, and re-layouts: 122 us -> none  [the longest x16 107 us: deposit(): return lax.dynamic_update_slice(buffer, current + addition, anchor)]
    another operation x13 -> x0, loops' own time: 100 us -> none  [the longest x2 61.1 us: backward_step(): gradient = lax.fori_loop(0, per_group, deposit, gradient)]
    ppermute x12 -> x0, starting transfers between devices: 66.5 us -> none  [the longest x4 49.5 us: from_behind(): return lax.ppermute(block, axis, route)]
    dot_general x16 -> x0, matrix products: 37.4 us -> none  [the longest x8 22.4 us: product(): return jnp.einsum('jk,bkl->bjl', matrix, data, precision=precise)]
    ppermute x12 -> x0, waiting for transfers between devices: 37.3 us -> none  [the longest x4 21.3 us: padded_2(): after = lax.ppermute(first, axis, down)]
    add x21 -> x1, other arithmetic: 37.3 us -> 0.01 us  [shards(): centres[0, 0].reshape(count, 2)]
  transfers between devices with their start and end apart: 13 -> 0, of which waited for: 7 -> 0; matrix products, arithmetic and copies ran while one was open for 20% -> 0% of each run, Pallas kernels for 0% -> 0%
where the time goes in v1:
time: 144 us
  Pallas kernels  136 us (94%)
  local copies, waits for them, and re-layouts  3.88 us (3%)
  other arithmetic  2.75 us (2%)
    pallas_call x1, Pallas kernels, send_back(): pl.pallas_call(return_kernel_flat, out_shape=tuple((jax.ShapeDtypeStruct(...  51.6 us
    pallas_call x1, Pallas kernels, exchange_halo(): pl.pallas_call(functools.partial(halo_kernel, rows, cols, halo), out_shap...  31.8 us
    pallas_call x1, Pallas kernels, waves(): pl.pallas_call(functools.partial(wave_kernel, half), out_shape=(jax.Shape...  25 us
    pallas_call x1, Pallas kernels, scatter(): pl.pallas_call(functools.partial(scatter_kernel, half, rows, cols, halo),...  9.04 us
    pallas_call x1, Pallas kernels, extract(): pl.pallas_call(functools.partial(extract_kernel, n, rows_all), out_shape=...  7.27 us
    pallas_call x2, Pallas kernels, swap(): pl.pallas_call(functools.partial(swap_kernel, count), out_shape=tuple((ja...  6.24 us
    pallas_call x1, Pallas kernels, fold(): pl.pallas_call(functools.partial(fold_kernel, halo), out_shape=(jax.Shape...  5.3 us

profile of v1, /device:TPU:0, one launch (start us, length us, event | category | flops | bytes accessed | tf_op | source)
XLA Modules:
  0.0 143.5 jit_solution(10571611964712864675)
XLA Ops:
  0.6 0.1 pad_add_fusion.1
  0.7 0.5 broadcast.9
  1.2 1.3 reduce.3
  2.5 0.1 lt.29
  2.6 0.1 add_bitcast_fusion
  2.7 0.1 lt.30
  2.8 0.1 lt.31
  2.9 0.1 lt.27
  3.0 0.6 pad_add_fusion.2.info_ref
  3.6 0.8 copy.25
  4.4 0.0 copy-start
  4.4 0.6 pad_add_fusion.at_ref
  5.0 31.8 %halo_in.1.pad_ref = bf16[2,640,1280]{2,1,0:T(8,128)(2,1)} custom-call(bf16[1,512,1024]{2,1,0:T(8,128)(2,1)} %re_ref.1, bf16[1,512,1024]{2,1,0:T(8,128)(2,1)} %im_ref.1), custom_call_target="tpu_custom_call" | custom-call | tf_op jit(solution)/shard_map/halo_in/pallas_call | solution.py:97
  36.8 0.0 copy-done
  36.8 7.3 %extract.1 = (bf16[4,2,256,256]{3,2,1,0:T(8,128)(2,1)}, bf16[4,2,256,256]{3,2,1,0:T(8,128)(2,1)}) custom-call(s32[8,2]{1,0:T(8,128)} %copy-done, bf16[2,640,1280]{2,1,0:T(8,128)(2,1)} %halo_in.1.pad_ref), custom_call_target="tpu_custom_call" | custom-call | tf_op jit(solution)/shard_map/extract/pallas_call | solution.py:162
  44.1 3.0 %swap_in.1.other_ref = bf16[4,2,256,256]{3,2,1,0:T(8,128)(2,1)} custom-call(bf16[4,2,256,256]{3,2,1,0:T(8,128)(2,1)} %get-tuple-element.18.refs_0_), custom_call_target="tpu_custom_call" | custom-call | tf_op jit(solution)/shard_map/swap_in/pallas_call | solution.py:193
  47.1 25.0 %waves.1 = (bf16[2,4,2,256,256]{4,3,2,1,0:T(8,128)(2,1)}, f32[2,128,256]{2,1,0:T(8,128)}, bf16[2,128,256]{2,1,0:T(8,128)(2,1)}) custom-call(s32[5]{0:T(128)} %pad_add_fusion.2.info_ref, f32[2,256,256]{2,1,0:T(8,128)} %probe_ref.1, f32[256,256]{1,0:T(8,128)} %phases_ref.1, bf16[8,256,256]{2,1,0:T(8,128)(2,1)} %constant.30.clone.mats_ref, ...), custom_call_target="tpu_custom_call" | custom-call | tf_op jit(solution)/shard_map/waves/pallas_call | solution.py:331
  72.1 2.3 %dynamic-slice_bitcast_fusion.refs_0_ = bf16[4,2,256,256]{3,2,1,0:T(8,128)(2,1)} fusion(bf16[2,4,2,256,256]{4,3,2,1,0:T(8,128)(2,1)} %get-tuple-element.19.mine_ref, s32[]{:T(128)S(6)} %select_n.28), kind=kLoop, calls=%fused_computation | loop fusion | bytes 2097156 | tf_op jit(solution)/shard_map/jit(dynamic_index_in_dim)/squeeze | solution.py:567
  74.4 3.2 %swap_out.1 = (bf16[4,2,256,256]{3,2,1,0:T(8,128)(2,1)}, bf16[2,128,256]{2,1,0:T(8,128)(2,1)}) custom-call(bf16[4,2,256,256]{3,2,1,0:T(8,128)(2,1)} %dynamic-slice_bitcast_fusion.refs_0_, bf16[2,128,256]{2,1,0:T(8,128)(2,1)} %get-tuple-element.20.refs_1_), custom_call_target="tpu_custom_call" | custom-call | tf_op jit(solution)/shard_map/swap_out/pallas_call | solution.py:193
  77.6 9.0 %scatter.1 = (f32[2,512,1024]{2,1,0:T(8,128)}, bf16[2,128,1024]{2,1,0:T(8,128)(2,1)}, bf16[2,2,512,128]{3,2,1,0:T(8,128)(2,1)}, bf16[2,2,128,128]{3,2,1,0:T(8,128)(2,1)}) custom-call(s32[9,2]{1,0:T(8,128)} %pad_add_fusion.at_ref, bf16[2,4,2,256,256]{4,3,2,1,0:T(8,128)(2,1)} %get-tuple-element.19.mine_ref, bf16[4,2,256,256]{3,2,1,0:T(8,128)(2,1)} %get-tuple-element.21.got_ref), custom_call_target="tpu_custom_call" | custom-call | tf_op jit(solution)/shard_map/scatter/pallas_call | solution.py:393
  86.7 51.6 %halo_out.1 = (bf16[2,128,1024]{2,1,0:T(8,128)(2,1)}, bf16[2,2,512,128]{3,2,1,0:T(8,128)(2,1)}, bf16[2,2,128,128]{3,2,1,0:T(8,128)(2,1)}, f32[64,8,128]{2,1,0:T(8,128)}) custom-call(bf16[2,128,1024]{2,1,0:T(8,128)(2,1)} %get-tuple-element.23.refs_0_, bf16[2,2,512,128]{3,2,1,0:T(8,128)(2,1)} %get-tuple-element.24.refs_1_, ...), custom_call_target="tpu_custom_call" | custom-call | tf_op jit(solution)/shard_map/halo_out/pallas_call | solution.py:496
  138.2 5.3 %fold.1 = (f32[2,1,512,1024]{3,2,1,0:T(8,128)}, f32[2,128,256]{2,1,0:T(8,128)}) custom-call(s32[1]{0:T(128)} %bitcast.info_ref, f32[2,512,1024]{2,1,0:T(8,128)} %get-tuple-element.22.centre_ref, bf16[2,128,1024]{2,1,0:T(8,128)(2,1)} %get-tuple-element.28.row_ref, bf16[2,2,512,128]{3,2,1,0:T(8,128)(2,1)} %get-tuple-element.29.side_ref, ...), custom_call_target="tpu_custom_call" | custom-call | tf_op jit(solution)/shard_map/fold/pallas_call | solution.py:541
  (6 shorter events, 0.0 us)
Async XLA Ops:
  4.4 32.4 %copy-start = (s32[8,2]{1,0:T(8,128)}, s32[8,2]{1,0:T(8,128)S(1)}, u32[]{:S(2)}) copy-start(s32[8,2]{1,0:T(8,128)S(1)} %add_select_fusion.at_ref) | copy-start | bytes 196

commit v2 on v1

v2 whole, which is shorter than its diff:
```python
import functools

import jax
import jax.numpy as jnp
import numpy as np
from jax import lax
from jax.experimental import pallas as pl
from jax.experimental.pallas import tpu as pltpu
from jax.sharding import PartitionSpec as P

MESH = pl.DeviceIdType.MESH
F32 = jnp.float32
BF16 = jnp.bfloat16
ANY = pl.BlockSpec(memory_space=pl.ANY)
LANE = 128
ORDER = ((), (0, 1), (2,), (3,))
REDUCE = True
NAME = 'halo_out'


def constants(n):
    half = n // 2
    k = np.arange(half)
    parts = []
    for parity in range(2):
        turns = (np.outer(2 * k + parity, k) % n) / n
        w = np.exp(-2j * np.pi * turns) / np.sqrt(n)
        block = np.block([[w.real, -w.imag], [w.imag, w.real]])
        for matrix in (block, block.T):
            high = matrix.astype(np.float32).astype(BF16)
            low = (matrix - high.astype(np.float64)).astype(np.float32).astype(BF16)
            parts += [high, low]
    order = np.concatenate([np.arange(0, n, 2), np.arange(1, n, 2)])
    perm = np.zeros((n, n), np.float32)
    perm[np.arange(n), order] = 1.0
    return np.stack(parts), np.stack([perm, perm.T]).astype(BF16)


def axis_ids():
    return lax.axis_index("depth"), lax.axis_index("row"), lax.axis_index("col")


def meet(peers):
    barrier = pltpu.get_barrier_semaphore()
    for peer in peers:
        pl.semaphore_signal(barrier, inc=1, device_id=peer, device_id_type=MESH)
    pl.semaphore_wait(barrier, len(peers))


def remote(src, dst, sems, slot, peer):
    return pltpu.make_async_remote_copy(
        src_ref=src, dst_ref=dst, send_sem=sems[0].at[slot], recv_sem=sems[1].at[slot], device_id=peer, device_id_type=MESH
    )


def neighbours():
    d, r, c = axis_ids()
    cols = lax.axis_size("col")
    right, left = lax.rem(c + 1, cols), lax.rem(c + cols - 1, cols)
    return [(d, 1 - r, c), (d, r, right), (d, r, left), (d, 1 - r, right), (d, 1 - r, left)]


def shifted_in(x, down, right):
    rows, cols = x.shape
    turned = pltpu.roll(x.reshape(rows // 8, 8, cols), jnp.bitwise_and(8 - down, 7), 1)
    sub = lax.broadcasted_iota(jnp.int32, (rows // 8 - 1, 8, cols), 1)
    x = jnp.where(sub < 8 - down, turned[:-1], turned[1:]).reshape(rows - 8, cols)
    turned = [pltpu.roll(x[:, i : i + LANE], jnp.bitwise_and(LANE - right, LANE - 1), 1) for i in range(0, cols, LANE)]
    lanes = lax.broadcasted_iota(jnp.int32, turned[0].shape, 1)
    return jnp.concatenate([jnp.where(lanes < LANE - right, a, b) for a, b in zip(turned[:-1], turned[1:])], 1)


def shifted_out(x, down, right):
    rows, cols = x.shape
    turned = [pltpu.roll(x[:, i : i + LANE], right, 1) for i in range(0, cols, LANE)]
    lanes = lax.broadcasted_iota(jnp.int32, turned[0].shape, 1)
    none = jnp.zeros_like(turned[0])
    x = jnp.concatenate([jnp.where(lanes < right, a, b) for a, b in zip([none] + turned, turned + [none])], 1)
    cols = cols + LANE
    turned = pltpu.roll(x.reshape(rows // 8, 8, cols), down, 1)
    none = jnp.zeros((1, 8, cols), x.dtype)
    sub = lax.broadcasted_iota(jnp.int32, (rows // 8 + 1, 8, cols), 1)
    both = jnp.where(sub < down, jnp.concatenate([none, turned], 0), jnp.concatenate([turned, none], 0))
    return both.reshape(rows + 8, cols)


def split(x):
    high = x.astype(BF16)
    return high, (x - high.astype(F32)).astype(BF16)


def product(a, b, passes):
    (ah, al), (bh, bl) = a, b
    if passes == 3:
        lhs, rhs = [ah, ah, al], [bh, bl, bh]
    else:
        lhs, rhs = [ah], [bh]
    lhs = jnp.concatenate(lhs, 1) if len(lhs) > 1 else lhs[0]
    rhs = jnp.concatenate(rhs, 0) if len(rhs) > 1 else rhs[0]
    return jnp.dot(lhs, rhs, preferred_element_type=F32)


def make_transforms(mats_ref):
    def mat(parity, transposed):
        at = parity * 4 + transposed * 2
        return mats_ref[at], mats_ref[at + 1]

    def forward(zr, zi):
        h = zr.shape[0] // 2
        outs = []
        for parity in range(2):
            fold = (lambda z: z[:h] + z[h:]) if parity == 0 else (lambda z: z[:h] - z[h:])
            outs.append(product(mat(parity, 0), split(jnp.concatenate([fold(zr), fold(zi)], 0)), 3))
        yr = jnp.concatenate([outs[0][:h], outs[1][:h]], 0)
        yi = jnp.concatenate([outs[0][h:], outs[1][h:]], 0)
        outs = []
        for parity in range(2):
            fold = (lambda z: z[:, :h] + z[:, h:]) if parity == 0 else (lambda z: z[:, :h] - z[:, h:])
            outs.append(product(split(jnp.concatenate([fold(yr), fold(yi)], 1)), mat(parity, 1), 3))
        return (
            jnp.concatenate([outs[0][:, :h], outs[1][:, :h]], 1),
            jnp.concatenate([outs[0][:, h:], outs[1][:, h:]], 1),
        )

    def inverse(zr, zi):
        h = zr.shape[0] // 2
        e = product(mat(0, 1), split(jnp.concatenate([zr[:h], zi[:h]], 0)), 3)
        o = product(mat(1, 1), split(jnp.concatenate([zr[h:], zi[h:]], 0)), 3)
        yr = jnp.concatenate([e[:h] + o[:h], e[:h] - o[:h]], 0)
        yi = jnp.concatenate([e[h:] + o[h:], e[h:] - o[h:]], 0)
        e = product(split(jnp.concatenate([yr[:, :h], yi[:, :h]], 1)), mat(0, 0), 3)
        o = product(split(jnp.concatenate([yr[:, h:], yi[:, h:]], 1)), mat(1, 0), 3)
        return (
            jnp.concatenate([e[:, :h] + o[:, :h], e[:, :h] - o[:, :h]], 1),
            jnp.concatenate([e[:, h:] + o[:, h:], e[:, h:] - o[:, h:]], 1),
        )

    return forward, inverse


def cmul(ar, ai, br, bi):
    return ar * br - ai * bi, ar * bi + ai * br


def conj_mul(ar, ai, br, bi):
    return ar * br + ai * bi, ar * bi - ai * br


def rounded(x):
    return x.astype(BF16).astype(F32)


def halo_kernel(half, halo, phases_ref, perm_ref, re_ref, im_ref, frames_ref, pad_ref, kern_ref, ready_ref, stage, frames, send, recv, own):
    d, r, _ = axis_ids()
    _, rows, cols = re_ref.shape
    slots = frames_ref.shape[3]
    batch = half // slots
    peers = neighbours()
    everything, first, last = pl.ds(0, rows), pl.ds(0, halo), pl.ds(cols - halo, halo)
    middle, before, after = pl.ds(halo, cols), pl.ds(0, halo), pl.ds(halo + cols, halo)
    edge = pl.ds(pl.multiple_of((rows - halo) * (1 - r), halo), halo)
    far = pl.ds(pl.multiple_of(rows * r, halo), halo)
    mine = pl.ds(pl.multiple_of(halo * r, halo), rows)
    loads = [pltpu.make_async_copy(src.at[0], stage.at[p], own.at[p]) for p, src in enumerate((re_ref, im_ref))]
    loads.append(pltpu.make_async_copy(frames_ref.at[0, 0, pl.ds(d * batch, batch)], frames, own.at[4]))
    for load in loads:
        load.start()
    meet(peers)
    moves = [
        (edge, pl.ds(0, cols), far, middle),
        (everything, last, mine, before),
        (everything, first, mine, after),
        (edge, last, far, before),
        (edge, first, far, after),
    ]
    copies = []
    for p, src in enumerate((re_ref, im_ref)):
        for i, (sr, sc, dr, dc) in enumerate(moves):
            copies.append(remote(src.at[0, sr, sc], pad_ref.at[p, dr, dc], (send, recv), p * 5 + i, peers[i]))
            copies[-1].start()
    stores = [pltpu.make_async_copy(stage.at[p], pad_ref.at[p, mine, middle], own.at[2 + p]) for p in range(2)]
    for load, store in zip(loads, stores):
        load.wait()
        store.start()
    kern_ref[0] = reorder(jnp.cos(phases_ref[...]), perm_ref, True)
    kern_ref[1] = reorder(jnp.sin(phases_ref[...]), perm_ref, True)
    loads[2].wait()

    @pl.loop(0, half)
    def _(k):
        ready_ref[k] = reorder(frames[k // slots, lax.rem(k, slots)], perm_ref, True)

    for store in stores:
        store.wait()
    for copy in copies:
        copy.wait()


def exchange_halo(object_re, object_im, phases, perm, measured, halo):
    _, rows, cols = object_re.shape
    batches, slots, n = measured.shape[2:5]
    half = batches * slots // 2
    vmem = pl.BlockSpec(memory_space=pltpu.VMEM)
    dma = pltpu.SemaphoreType.DMA
    return pl.pallas_call(
        functools.partial(halo_kernel, half, halo),
        out_shape=(
            jax.ShapeDtypeStruct((2, rows + halo, cols + 2 * halo), BF16),
            jax.ShapeDtypeStruct((2, n, n), F32),
            jax.ShapeDtypeStruct((half, n, n), F32),
        ),
        in_specs=[vmem, vmem, ANY, ANY, ANY],
        out_specs=(ANY, vmem, vmem),
        scratch_shapes=[
            pltpu.VMEM((2, rows, cols), BF16),
            pltpu.VMEM((half // slots, slots, n, n), F32),
            dma((10,)), dma((10,)), dma((5,)),
        ],
        compiler_params=pltpu.CompilerParams(collective_id=0, has_side_effects=True),
        name="halo_in",
    )(phases, perm, object_re, object_im, measured)


def extract_kernel(halo, centres, occupied, pad_ref, mine_ref, theirs_ref, pieces, wide, load, store, done):
    d, r, _ = axis_ids()
    count = pieces.shape[0]
    half = count // 2
    n = done.shape[-1]
    tall = n + 16
    rows_all = pad_ref.shape[1]
    slots = centres.shape[3]

    def place(k):
        at = jnp.where(k < half, (1 - d) * half + k, d * half + k - half)
        batch, slot = at // slots, lax.rem(at, slots)
        row = centres[0, 0, batch, slot, 0] + halo * (r - 1)
        col = centres[0, 0, batch, slot, 1]
        base = pl.multiple_of(jnp.minimum(row // 16 * 16, rows_all - tall), 16)
        lane = pl.multiple_of(col // LANE * LANE, LANE)
        return base, lane, row - base, col - lane, slot < occupied[0, 0, batch]

    def piece_load(k):
        base, lane, _, _, _ = place(k)
        return pltpu.make_async_copy(pad_ref.at[:, pl.ds(base, tall), pl.ds(lane, n + LANE)], pieces.at[k], load.at[k])

    @pl.loop(0, count)
    def _(k):
        piece_load(k).start()

    def cut(k):
        piece_load(k).wait()
        _, _, down, right, live = place(k)
        skip = pl.multiple_of(down // 8 * 8, 8)
        for p in range(2):
            wide[p, pl.ds(0, tall), :] = pieces[k, p].astype(F32)
            window = shifted_in(wide[p, pl.ds(skip, n + 8), :], down - skip, right)
            done[k, p] = jnp.where(live, window, 0.0).astype(BF16)

    for part, out in enumerate((theirs_ref, mine_ref)):
        @pl.loop(0, half)
        def _(k):
            cut(part * half + k)
            pltpu.make_async_copy(done.at[part * half + k], out.at[k], store.at[part * half + k]).start()

    for part, out in enumerate((theirs_ref, mine_ref)):
        for k in range(half):
            pltpu.make_async_copy(done.at[part * half + k], out.at[k], store.at[part * half + k]).wait()


def extract(centres, occupied, padded, n):
    count = occupied.shape[2] * centres.shape[3]
    half = count // 2
    shape = jax.ShapeDtypeStruct((half, 2, n, n), BF16)
    smem = pl.BlockSpec(memory_space=pltpu.SMEM)
    return pl.pallas_call(
        functools.partial(extract_kernel, n // 2),
        out_shape=(shape, shape),
        in_specs=[smem, smem, ANY],
        out_specs=(ANY, ANY),
        scratch_shapes=[
            pltpu.VMEM((count, 2, n + 16, n + LANE), BF16),
            pltpu.VMEM((2, n + 24, n + LANE), F32),
            pltpu.SemaphoreType.DMA((count,)),
            pltpu.SemaphoreType.DMA((count,)),
            pltpu.VMEM((count, 2, n, n), BF16),
        ],
        name="extract",
    )(centres, occupied, padded)


def reorder(x, perm_ref, both):
    high, low = split(x)
    if both:
        high = jnp.dot(perm_ref[0], high, preferred_element_type=F32).astype(BF16)
        low = jnp.dot(perm_ref[0], low, preferred_element_type=F32).astype(BF16)
    return jnp.dot(high, perm_ref[1], preferred_element_type=F32) + jnp.dot(low, perm_ref[1], preferred_element_type=F32)


def wave_kernel(
    half, probe_ref, kern, mats_ref, mine_ref, theirs_ref, frames_ref,
    terms_ref, keep_ref, given_ref,
    windows, frames, grads, total, give, own_sem, frame_sem, swap_send, swap_recv, term_send, term_recv, term_own, give_send, give_recv,
):
    d, r, c = axis_ids()
    n = probe_ref.shape[1]
    partner = (1 - d, r, c)

    def own_copy(k):
        return pltpu.make_async_copy(mine_ref.at[k], windows.at[d, k], own_sem.at[k])

    def frame_copy(k):
        return pltpu.make_async_copy(frames_ref.at[k], frames.at[k], frame_sem.at[k])

    def window_copy(k):
        return remote(theirs_ref.at[k], windows.at[d, k], (swap_send, swap_recv), k, partner)

    def term_copies(k):
        there = terms_ref.at[d * half + k]
        return (
            remote(grads.at[1 - d, k], there, (term_send, term_recv), k, partner),
            pltpu.make_async_copy(grads.at[d, k], there, term_own.at[k]),
        )

    @pl.loop(0, half)
    def _(k):
        own_copy(k).start()
        frame_copy(k).start()

    meet([partner])

    @pl.loop(0, half)
    def _(k):
        window_copy(k).start()

    total[...] = jnp.zeros_like(total)
    forward, inverse = make_transforms(mats_ref)

    @pl.loop(0, half)
    def _(k):
        def window(s):
            return [windows[s, k, p].astype(F32) for p in range(2)]

        own_copy(k).wait()
        frame_copy(k).wait()
        window_copy(k).wait()
        fr, fi = forward(*cmul(probe_ref[0], probe_ref[1], *window(0)))
        pr, pi = inverse(*cmul(fr, fi, kern[0], kern[1]))
        pr, pi = rounded(pr), rounded(pi)
        w1r, w1i = window(1)
        fr, fi = forward(*cmul(pr, pi, w1r, w1i))
        misfit = fr * fr + fi * fi - frames[k]
        xr, xi = inverse(misfit * fr, misfit * fi)
        gr, gi = conj_mul(pr, pi, xr, xi)
        grads[1, k, 0] = gr.astype(BF16)
        grads[1, k, 1] = gi.astype(BF16)
        fr, fi = forward(*conj_mul(w1r, w1i, xr, xi))
        xr, xi = inverse(*conj_mul(kern[0], kern[1], fr, fi))
        xr, xi = rounded(xr), rounded(xi)
        gr, gi = conj_mul(probe_ref[0], probe_ref[1], xr, xi)
        grads[0, k, 0] = gr.astype(BF16)
        grads[0, k, 1] = gi.astype(BF16)
        lr, li = conj_mul(*window(0), xr, xi)
        total[0] += lr
        total[1] += li
        for copy in term_copies(k):
            copy.start()

    mid = n // 2
    for p in range(2):
        give[p] = total[p, pl.ds(pl.multiple_of((1 - d) * mid, 8), mid), :].astype(BF16)
        keep_ref[p] = total[p, pl.ds(pl.multiple_of(d * mid, 8), mid), :]
    last_copy = pltpu.make_async_remote_copy(give, given_ref, give_send, give_recv, device_id=partner, device_id_type=MESH)
    last_copy.start()

    @pl.loop(0, half)
    def _(k):
        for copy in term_copies(k):
            copy.wait()

    last_copy.wait()


def waves(probe, kern, mats, mine, theirs, frames):
    half, _, n, _ = mine.shape
    vmem = pl.BlockSpec(memory_space=pltpu.VMEM)
    dma = pltpu.SemaphoreType.DMA
    return pl.pallas_call(
        functools.partial(wave_kernel, half),
        out_shape=(
            jax.ShapeDtypeStruct((2 * half, 2, n, n), BF16),
            jax.ShapeDtypeStruct((2, n // 2, n), F32),
            jax.ShapeDtypeStruct((2, n // 2, n), BF16),
        ),
        in_specs=[vmem, vmem, vmem, ANY, ANY, ANY],
        out_specs=(ANY, vmem, ANY),
        scratch_shapes=[
            pltpu.VMEM((2, half, 2, n, n), BF16),
            pltpu.VMEM((half, n, n), F32),
            pltpu.VMEM((2, half, 2, n, n), BF16),
            pltpu.VMEM((2, n, n), F32),
            pltpu.VMEM((2, n // 2, n), BF16),
        ]
        + [dma((half,))] * 7 + [dma(()), dma(())],
        compiler_params=pltpu.CompilerParams(collective_id=1, has_side_effects=True),
        name="waves",
    )(probe, kern, mats, mine, theirs, frames)


def scatter_kernel(halo, centres, terms_ref, centre_ref, row_ref, side_ref, corner_ref, terms, acc, load, store):
    _, r, _ = axis_ids()
    count, _, n, _ = terms.shape
    _, _, rows, cols = centre_ref.shape
    slots = centres.shape[3]

    def term_load(k):
        return pltpu.make_async_copy(terms_ref.at[k], terms.at[k], load.at[k])

    for k in range(count):
        term_load(k).start()
    acc[...] = jnp.zeros_like(acc)

    @pl.loop(0, count)
    def _(k):
        term_load(k).wait()
        row = centres[0, 0, k // slots, lax.rem(k, slots), 0] + halo * (r - 1)
        col = centres[0, 0, k // slots, lax.rem(k, slots), 1]
        top = pl.multiple_of(row // 8 * 8, 8)
        lane = pl.multiple_of(col // LANE * LANE, LANE)
        for p in range(2):
            acc[p, pl.ds(top, n + 8), pl.ds(lane, n + LANE)] += shifted_out(terms[k, p].astype(F32), row - top, col - lane)

    mine = pl.ds(pl.multiple_of(halo * r, halo), rows)
    far = pl.ds(pl.multiple_of(rows * (1 - r), halo), halo)
    stores = [pltpu.make_async_copy(acc.at[p, mine, pl.ds(halo, cols)], centre_ref.at[p, 0], store.at[p]) for p in range(2)]
    for copy in stores:
        copy.start()
    for p in range(2):
        row_ref[p] = acc[p, far, pl.ds(halo, cols)].astype(BF16)
        for i, at in enumerate((halo + cols, 0)):
            side_ref[i, p] = acc[p, mine, pl.ds(at, halo)].astype(BF16)
            corner_ref[i, p] = acc[p, far, pl.ds(at, halo)].astype(BF16)
    for copy in stores:
        copy.wait()


def scatter(centres, terms, rows, cols, halo):
    count, _, n, _ = terms.shape
    vmem = pl.BlockSpec(memory_space=pltpu.VMEM)
    shapes = [((2, 1, rows, cols), F32), ((2, halo, cols), BF16), ((2, 2, rows, halo), BF16), ((2, 2, halo, halo), BF16)]
    return pl.pallas_call(
        functools.partial(scatter_kernel, halo),
        out_shape=tuple(jax.ShapeDtypeStruct(s, t) for s, t in shapes),
        in_specs=[pl.BlockSpec(memory_space=pltpu.SMEM), ANY],
        out_specs=(ANY, vmem, vmem, vmem),
        scratch_shapes=[
            pltpu.VMEM(terms.shape, BF16),
            pltpu.VMEM((2, rows + halo + 8, cols + 2 * halo), F32),
            pltpu.SemaphoreType.DMA((count,)),
            pltpu.SemaphoreType.DMA((2,)),
        ],
        name="scatter",
    )(centres, terms)


def x_peer(q):
    d, _, c = axis_ids()
    return (d, q // 2, c // 2 * 2 + lax.rem(q, 2))


def plane_peer(q):
    d, r, c = axis_ids()
    return (d, r, q * 2 + lax.rem(c, 2))


def return_kernel(row_ref, side_ref, corner_ref, keep_ref, got_ref, row_out, side_out, corner_out, probe_out, buf, line, plane, strips, xs, ps, gs):
    d, r, c = axis_ids()
    planes = lax.axis_size("col") // 2
    my_x = r * 2 + lax.rem(c, 2)
    my_p = c // 2
    peers = neighbours()
    line_peers = [lax.rem(my_x + t, 4) for t in range(1, 4)]
    plane_peers = [lax.rem(my_p + t, planes) for t in range(1, planes)]
    meet(peers + [x_peer(q) for q in line_peers] + [plane_peer(q) for q in plane_peers])
    wide = row_ref.shape[-1] // 2
    groups = [[] for _ in range(4)]
    for p in range(2):
        for i in range(2):
            part = (p, slice(None), pl.ds(i * wide, wide))
            groups[2 * p + i].append((row_ref.at[part], row_out.at[part], peers[0]))
            groups[2 * p + i].append((side_ref.at[i, p], side_out.at[i, p], peers[1 + i]))
            groups[2 * p + i].append((corner_ref.at[i, p], corner_out.at[i, p], peers[3 + i]))
    copies = []

    def launch(chosen):
        for s, t, peer in [m for g in chosen for m in groups[g]]:
            copies.append(remote(s, t, strips, len(copies), peer))
            copies[-1].start()

    half_rows, n = keep_ref.shape[1:]
    at = 0
    for p in range(2):
        for t in range(half_rows // 8):
            for h in range(n // LANE):
                place = (p, pl.ds(8 * t, 8), pl.ds(LANE * h, LANE))
                buf[at] = keep_ref[place] + got_ref[place].astype(F32)
                at += 1
    share = at // planes

    def piece(ref, q):
        return ref.at[pl.ds(q * share, share)]

    def send(src, dst, sems, q, me, peer):
        copy = pltpu.make_async_remote_copy(src, dst, sems[0].at[q], sems[1].at[me], device_id=peer, device_id_type=MESH)
        copy.start()
        sent.append(copy)

    def receive(dst, sems, q, peer):
        pltpu.make_async_remote_copy(dst, dst, sems[0].at[q], sems[1].at[q], device_id=peer, device_id_type=MESH).wait_recv()

    sent = []
    launch(ORDER[0])
    for q in plane_peers:
        send(piece(buf, q), plane.at[my_p], ps, q, my_p, plane_peer(q))
    launch(ORDER[1])
    for q in plane_peers:
        receive(plane.at[q], ps, q, plane_peer(q))
    total = buf[pl.ds(my_p * share, share)]
    for q in plane_peers:
        total = total + plane[q]
    line[my_x] = total
    for q in line_peers:
        send(line.at[my_x], line.at[my_x], xs, q, my_x, x_peer(q))
    launch(ORDER[2])
    for q in line_peers:
        receive(line.at[q], xs, q, x_peer(q))
    probe_out[pl.ds(my_p * share, share)] = (line[0] + line[1]) + (line[2] + line[3])
    for q in plane_peers:
        send(piece(probe_out, my_p), piece(probe_out, my_p), gs, q, my_p, plane_peer(q))
    launch(ORDER[3])
    for q in plane_peers:
        receive(piece(probe_out, q), gs, q, plane_peer(q))
    for copy in sent:
        copy.wait_send()
    for copy in copies:
        copy.wait()


def send_back(row, side, corner, keep, got):
    chunks = keep.size // (8 * LANE)
    planes = lax.axis_size("col") // 2
    share = chunks // planes
    vmem = pl.BlockSpec(memory_space=pltpu.VMEM)
    dma = lambda n: [pltpu.SemaphoreType.DMA((n,)), pltpu.SemaphoreType.DMA((n,))]
    return pl.pallas_call(
        return_kernel_flat,
        out_shape=tuple(jax.ShapeDtypeStruct(a.shape, a.dtype) for a in (row, side, corner)) + (jax.ShapeDtypeStruct((chunks, 8, LANE), F32),),
        in_specs=[ANY, ANY, ANY, vmem, vmem],
        out_specs=(ANY, ANY, ANY, vmem),
        scratch_shapes=[
            pltpu.VMEM((chunks, 8, LANE), F32),
            pltpu.VMEM((4, share, 8, LANE), F32),
            pltpu.VMEM((planes, share, 8, LANE), F32),
        ]
        + dma(12) + dma(4) + dma(planes) + dma(planes),
        compiler_params=pltpu.CompilerParams(collective_id=3, has_side_effects=True),
        name=NAME,
    )(row, side, corner, keep, got)


def return_kernel_flat(*refs):
    sems = refs[12:]
    return_kernel(*refs[:12], *[sems[i : i + 2] for i in range(0, 8, 2)])


def fold_kernel(halo, centre_ref, row_ref, side_ref, corner_ref, chunks_ref, out_ref, probe_ref, sides, middle, load, store):
    _, r, _ = axis_ids()
    _, _, rows, cols = out_ref.shape
    edge = pl.ds(pl.multiple_of((rows - halo) * (1 - r), halo), halo)
    inner = pl.ds(halo, cols - 2 * halo)
    places = []
    for p in range(2):
        places.append((out_ref.at[p, 0, edge, inner], middle.at[p]))
        for i in range(2):
            places.append((out_ref.at[p, 0, :, pl.ds(i * (cols - halo), halo)], sides.at[i, p]))
    loads = [pltpu.make_async_copy(a, b, load.at[j]) for j, (a, b) in enumerate(places)]
    stores = [pltpu.make_async_copy(b, a, store.at[j]) for j, (a, b) in enumerate(places)]
    for copy in loads:
        copy.start()
    at = 0
    _, half_rows, n = probe_ref.shape
    for p in range(2):
        for t in range(half_rows // 8):
            for h in range(n // LANE):
                probe_ref[p, pl.ds(8 * t, 8), pl.ds(LANE * h, LANE)] = chunks_ref[at]
                at += 1
    for p in range(2):
        loads[3 * p].wait()
        middle[p] += row_ref[p, :, inner].astype(F32)
        stores[3 * p].start()
        for i in range(2):
            loads[3 * p + 1 + i].wait()
            sides[i, p] += side_ref[i, p].astype(F32)
            sides[i, p, edge, :] += row_ref[p, :, pl.ds(i * (cols - halo), halo)].astype(F32) + corner_ref[i, p].astype(F32)
            stores[3 * p + 1 + i].start()
    for copy in stores:
        copy.wait()


def fold(centre, row, side, corner, chunks, n):
    halo = row.shape[1]
    _, _, rows, cols = centre.shape
    vmem = pl.BlockSpec(memory_space=pltpu.VMEM)
    return pl.pallas_call(
        functools.partial(fold_kernel, halo),
        out_shape=(jax.ShapeDtypeStruct(centre.shape, F32), jax.ShapeDtypeStruct((2, n // 2, n), F32)),
        in_specs=[ANY, vmem, vmem, vmem, vmem],
        out_specs=(ANY, vmem),
        scratch_shapes=[
            pltpu.VMEM((2, 2, rows, halo), F32),
            pltpu.VMEM((2, halo, cols - 2 * halo), F32),
            pltpu.SemaphoreType.DMA((6,)),
            pltpu.SemaphoreType.DMA((6,)),
        ],
        input_output_aliases={0: 0},
        name="fold",
    )(centre, row, side, corner, chunks)


def shards(probe, object_re, object_im, phases, centres, occupied, measured):
    n = probe.shape[1]
    _, rows, cols = object_re.shape
    mats, perm = (jnp.asarray(x) for x in constants(n))
    padded, kern, frames = exchange_halo(object_re, object_im, phases, perm, measured, n // 2)
    mine, theirs = extract(centres, occupied, padded, n)
    terms, keep, given = waves(probe, kern, mats, mine, theirs, frames)
    centre, row, side, corner = scatter(centres, terms, rows, cols, n // 2)
    row, side, corner, chunks = send_back(row, side, corner, keep, given)
    return fold(centre, row, side, corner, chunks, n)


def solution(mesh):
    in_specs = (
        P(),
        P("depth", "row", "col"),
        P("depth", "row", "col"),
        P(),
        P("row", "col", None, None, None),
        P("row", "col", None),
        P("row", "col", None, None, None, None),
    )
    out_specs = (P(None, "depth", "row", "col"), P(None, "depth", None))
    return jax.shard_map(shards, mesh=mesh, in_specs=in_specs, out_specs=out_specs, check_vma=False)
```

time: 144 us -> 110 us (0.76)
  Pallas kernels: 136 us -> 107 us
  other arithmetic: 2.75 us -> 0 us
  local copies, waits for them, and re-layouts: 3.88 us -> 1.36 us
    pallas_call x1, Pallas kernels: 51.6 us -> 34.6 us  [send_back(): pl.pallas_call(return_kernel_flat, out_shape=tuple((jax.ShapeDtypeStruct(...]
    pallas_call x5 -> x3, Pallas kernels: 54.3 us -> 45.1 us  [the longest x1 34 us: exchange_halo(): pl.pallas_call(functools.partial(halo_kernel, half, halo), out_shape=(jax...]
    squeeze x1 -> x0, local copies, waits for them, and re-layouts: 2.26 us -> none  [shards(): away = lax.dynamic_index_in_dim(grads, 1 - d, 0, False)]
    pallas_call x1, Pallas kernels: 25 us -> 23.5 us  [waves(): pl.pallas_call(functools.partial(wave_kernel, half), out_shape=(jax.Shape...]
where the time goes in v2:
time: 110 us
  Pallas kernels  107 us (97%)
  local copies, waits for them, and re-layouts  1.36 us (1%)
    pallas_call x1, Pallas kernels, send_back(): pl.pallas_call(return_kernel_flat, out_shape=tuple((jax.ShapeDtypeStruct(...  34.6 us
    pallas_call x1, Pallas kernels, exchange_halo(): pl.pallas_call(functools.partial(halo_kernel, half, halo), out_shape=(jax...  34 us
    pallas_call x1, Pallas kernels, waves(): pl.pallas_call(functools.partial(wave_kernel, half), out_shape=(jax.Shape...  23.5 us
    pallas_call x1, Pallas kernels, scatter(): pl.pallas_call(functools.partial(scatter_kernel, halo), out_shape=tuple((...  6.44 us
    pallas_call x1, Pallas kernels, extract(): pl.pallas_call(functools.partial(extract_kernel, n // 2), out_shape=(shap...  4.67 us
    pallas_call x1, Pallas kernels, fold(): pl.pallas_call(functools.partial(fold_kernel, halo), out_shape=(jax.Shape...  4.38 us

profile of v2, /device:TPU:0, one launch (start us, length us, event | category | flops | bytes accessed | tf_op | source)
XLA Modules:
  0.0 109.5 jit_solution(80507598819629173)
XLA Ops:
  0.6 1.4 %copy.13.centres = s32[1,1,4,2,2]{4,3,2,1,0:T(2,128)} copy(s32[1,1,4,2,2]{2,4,3,1,0:T(2,128)} %param.13) | data formatting | bytes 128 | tf_op args[4]
  2.0 34.0 %halo_in.1 = (bf16[2,640,1280]{2,1,0:T(8,128)(2,1)}, f32[2,256,256]{2,1,0:T(8,128)}, f32[4,256,256]{2,1,0:T(8,128)}) custom-call(f32[256,256]{1,0:T(8,128)} %phases_ref.1, bf16[2,256,256]{2,1,0:T(8,128)(2,1)} %constant.5.clone.perm_ref, bf16[1,512,1024]{2,1,0:T(8,128)(2,1)} %re_ref.1, bf16[1,512,1024]{2,1,0:T(8,128)(2,1)} %im_ref.1, ...), custom_call_target="tpu_custom_call" | custom-call | tf_op jit(solution)/shard_map/halo_in/pallas_call | solution.py:205
  36.0 4.7 %extract.1 = (bf16[4,2,256,256]{3,2,1,0:T(8,128)(2,1)}, bf16[4,2,256,256]{3,2,1,0:T(8,128)(2,1)}) custom-call(s32[1,1,4,2,2]{4,3,2,1,0:T(2,128)} %copy.13.centres, s32[1,1,4]{2,1,0:T(1,128)} %occupied.1, bf16[2,640,1280]{2,1,0:T(8,128)(2,1)} %get-tuple-element.19.pad_ref), custom_call_target="tpu_custom_call" | custom-call | tf_op jit(solution)/shard_map/extract/pallas_call | solution.py:275
  40.6 23.5 %waves.1 = (bf16[8,2,256,256]{3,2,1,0:T(8,128)(2,1)}, f32[2,128,256]{2,1,0:T(8,128)}, bf16[2,128,256]{2,1,0:T(8,128)(2,1)}) custom-call(f32[2,256,256]{2,1,0:T(8,128)} %probe_ref.1, f32[2,256,256]{2,1,0:T(8,128)} %get-tuple-element.18.kern, bf16[8,256,256]{2,1,0:T(8,128)(2,1)} %constant.4.clone.mats_ref, ...), custom_call_target="tpu_custom_call" | custom-call | tf_op jit(solution)/shard_map/waves/pallas_call | solution.py:387
  64.1 6.4 %scatter.1 = (f32[2,1,512,1024]{3,2,1,0:T(8,128)}, bf16[2,128,1024]{2,1,0:T(8,128)(2,1)}, bf16[2,2,512,128]{3,2,1,0:T(8,128)(2,1)}, bf16[2,2,128,128]{3,2,1,0:T(8,128)(2,1)}) custom-call(s32[1,1,4,2,2]{4,3,2,1,0:T(2,128)} %copy.13.centres, bf16[8,2,256,256]{3,2,1,0:T(8,128)(2,1)} %get-tuple-element.23.terms_ref), custom_call_target="tpu_custom_call" | custom-call | tf_op jit(solution)/shard_map/scatter/pallas_call | solution.py:450
  70.6 34.6 %halo_out.1 = (bf16[2,128,1024]{2,1,0:T(8,128)(2,1)}, bf16[2,2,512,128]{3,2,1,0:T(8,128)(2,1)}, bf16[2,2,128,128]{3,2,1,0:T(8,128)(2,1)}, f32[64,8,128]{2,1,0:T(8,128)}) custom-call(bf16[2,128,1024]{2,1,0:T(8,128)(2,1)} %get-tuple-element.25.refs_0_, bf16[2,2,512,128]{3,2,1,0:T(8,128)(2,1)} %get-tuple-element.26.refs_1_, ...), custom_call_target="tpu_custom_call" | custom-call | tf_op jit(solution)/shard_map/halo_out/pallas_call | solution.py:554
  105.1 4.4 %fold.1 = (f32[2,1,512,1024]{3,2,1,0:T(8,128)}, f32[2,128,256]{2,1,0:T(8,128)}) custom-call(f32[2,1,512,1024]{3,2,1,0:T(8,128)} %get-tuple-element.24.centre_ref, bf16[2,128,1024]{2,1,0:T(8,128)(2,1)} %get-tuple-element.30.row_ref, bf16[2,2,512,128]{3,2,1,0:T(8,128)(2,1)} %get-tuple-element.31.side_ref, ...), custom_call_target="tpu_custom_call", output_to_operand_aliasing={{0}: (0, {})} | custom-call | tf_op jit(solution)/shard_map/fold/pallas_call | solution.py:613

commit v3 on v2

--- a/solution.py
+++ b/solution.py
@@ -105,35 +105,34 @@
         at = parity * 4 + transposed * 2
         return mats_ref[at], mats_ref[at + 1]
 
-    def forward(zr, zi):
-        h = zr.shape[0] // 2
-        outs = []
-        for parity in range(2):
-            fold = (lambda z: z[:h] + z[h:]) if parity == 0 else (lambda z: z[:h] - z[h:])
-            outs.append(product(mat(parity, 0), split(jnp.concatenate([fold(zr), fold(zi)], 0)), 3))
-        yr = jnp.concatenate([outs[0][:h], outs[1][:h]], 0)
-        yi = jnp.concatenate([outs[0][h:], outs[1][h:]], 0)
-        outs = []
-        for parity in range(2):
-            fold = (lambda z: z[:, :h] + z[:, h:]) if parity == 0 else (lambda z: z[:, :h] - z[:, h:])
-            outs.append(product(split(jnp.concatenate([fold(yr), fold(yi)], 1)), mat(parity, 1), 3))
-        return (
-            jnp.concatenate([outs[0][:, :h], outs[1][:, :h]], 1),
-            jnp.concatenate([outs[0][:, h:], outs[1][:, h:]], 1),
-        )
-
-    def inverse(zr, zi):
-        h = zr.shape[0] // 2
-        e = product(mat(0, 1), split(jnp.concatenate([zr[:h], zi[:h]], 0)), 3)
-        o = product(mat(1, 1), split(jnp.concatenate([zr[h:], zi[h:]], 0)), 3)
-        yr = jnp.concatenate([e[:h] + o[:h], e[:h] - o[:h]], 0)
-        yi = jnp.concatenate([e[h:] + o[h:], e[h:] - o[h:]], 0)
-        e = product(split(jnp.concatenate([yr[:, :h], yi[:, :h]], 1)), mat(0, 0), 3)
-        o = product(split(jnp.concatenate([yr[:, h:], yi[:, h:]], 1)), mat(1, 0), 3)
-        return (
-            jnp.concatenate([e[:, :h] + o[:, :h], e[:, :h] - o[:, :h]], 1),
-            jnp.concatenate([e[:, h:] + o[:, h:], e[:, h:] - o[:, h:]], 1),
-        )
+    def left(z, parity, transposed):
+        return product(mat(parity, transposed), split(jnp.concatenate(z, 0)), 3)
+
+    def right(z, parity, transposed):
+        return product(split(jnp.concatenate(z, 1)), mat(parity, transposed), 3)
+
+    def halves(z):
+        h = z.shape[0] // 2
+        return z[:h], z[h:]
+
+    def sides(z):
+        h = z.shape[1] // 2
+        return z[:, :h], z[:, h:]
+
+    def fold(parts, parity):
+        return parts[0] + parts[1] if parity == 0 else parts[0] - parts[1]
+
+    def forward(fields):
+        outs = [[left([fold(halves(x), parity) for x in z], parity, 0) for parity in range(2)] for z in fields]
+        fields = [[jnp.concatenate([halves(o)[i] for o in out], 0) for i in range(2)] for out in outs]
+        outs = [[right([fold(sides(x), parity) for x in z], parity, 1) for parity in range(2)] for z in fields]
+        return [[jnp.concatenate([sides(o)[i] for o in out], 1) for i in range(2)] for out in outs]
+
+    def inverse(fields):
+        outs = [[left([halves(x)[parity] for x in z], parity, 1) for parity in range(2)] for z in fields]
+        fields = [[jnp.concatenate([fold([halves(o)[i] for o in out], q) for q in range(2)], 0) for i in range(2)] for out in outs]
+        outs = [[right([sides(x)[parity] for x in z], parity, 0) for parity in range(2)] for z in fields]
+        return [[jnp.concatenate([fold([sides(o)[i] for o in out], q) for q in range(2)], 1) for i in range(2)] for out in outs]
 
     return forward, inverse
 
@@ -150,7 +149,7 @@
     return x.astype(BF16).astype(F32)
 
 
-def halo_kernel(half, halo, phases_ref, perm_ref, re_ref, im_ref, frames_ref, pad_ref, kern_ref, ready_ref, stage, frames, send, recv, own):
+def halo_kernel(half, halo, phases_ref, perm_ref, re_ref, im_ref, frames_ref, pad_ref, kern_ref, ready_ref, stage, frames, phases, perm, kern, ready, send, recv, own):
     d, r, _ = axis_ids()
     _, rows, cols = re_ref.shape
     slots = frames_ref.shape[3]
@@ -161,10 +160,6 @@
     edge = pl.ds(pl.multiple_of((rows - halo) * (1 - r), halo), halo)
     far = pl.ds(pl.multiple_of(rows * r, halo), halo)
     mine = pl.ds(pl.multiple_of(halo * r, halo), rows)
-    loads = [pltpu.make_async_copy(src.at[0], stage.at[p], own.at[p]) for p, src in enumerate((re_ref, im_ref))]
-    loads.append(pltpu.make_async_copy(frames_ref.at[0, 0, pl.ds(d * batch, batch)], frames, own.at[4]))
-    for load in loads:
-        load.start()
     meet(peers)
     moves = [
         (edge, pl.ds(0, cols), far, middle),
@@ -178,18 +173,38 @@
         for i, (sr, sc, dr, dc) in enumerate(moves):
             copies.append(remote(src.at[0, sr, sc], pad_ref.at[p, dr, dc], (send, recv), p * 5 + i, peers[i]))
             copies[-1].start()
-    stores = [pltpu.make_async_copy(stage.at[p], pad_ref.at[p, mine, middle], own.at[2 + p]) for p in range(2)]
-    for load, store in zip(loads, stores):
+    sources = [
+        (phases_ref, phases),
+        (perm_ref, perm),
+        (frames_ref.at[0, 0, pl.ds(d * batch, batch)], frames),
+        (re_ref.at[0], stage.at[0]),
+        (im_ref.at[0], stage.at[1]),
+    ]
+    targets = [
+        (kern, kern_ref),
+        (ready, ready_ref),
+        (stage.at[0], pad_ref.at[0, mine, middle]),
+        (stage.at[1], pad_ref.at[1, mine, middle]),
+    ]
+    loads = [pltpu.make_async_copy(a, b, own.at[i]) for i, (a, b) in enumerate(sources)]
+    stores = [pltpu.make_async_copy(a, b, own.at[5 + i]) for i, (a, b) in enumerate(targets)]
+    for load in loads:
+        load.start()
+    loads[0].wait()
+    loads[1].wait()
+    kern[0] = reorder(jnp.cos(phases[...]), perm, True)
+    kern[1] = reorder(jnp.sin(phases[...]), perm, True)
+    stores[0].start()
+    for load, store in zip(loads[3:], stores[2:]):
         load.wait()
         store.start()
-    kern_ref[0] = reorder(jnp.cos(phases_ref[...]), perm_ref, True)
-    kern_ref[1] = reorder(jnp.sin(phases_ref[...]), perm_ref, True)
     loads[2].wait()
 
     @pl.loop(0, half)
     def _(k):
-        ready_ref[k] = reorder(frames[k // slots, lax.rem(k, slots)], perm_ref, True)
-
+        ready[k] = reorder(frames[k // slots, lax.rem(k, slots)], perm, True)
+
+    stores[1].start()
     for store in stores:
         store.wait()
     for copy in copies:
@@ -200,7 +215,6 @@
     _, rows, cols = object_re.shape
     batches, slots, n = measured.shape[2:5]
     half = batches * slots // 2
-    vmem = pl.BlockSpec(memory_space=pltpu.VMEM)
     dma = pltpu.SemaphoreType.DMA
     return pl.pallas_call(
         functools.partial(halo_kernel, half, halo),
@@ -209,12 +223,16 @@
             jax.ShapeDtypeStruct((2, n, n), F32),
             jax.ShapeDtypeStruct((half, n, n), F32),
         ),
-        in_specs=[vmem, vmem, ANY, ANY, ANY],
-        out_specs=(ANY, vmem, vmem),
+        in_specs=[ANY] * 5,
+        out_specs=(ANY,) * 3,
         scratch_shapes=[
             pltpu.VMEM((2, rows, cols), BF16),
             pltpu.VMEM((half // slots, slots, n, n), F32),
-            dma((10,)), dma((10,)), dma((5,)),
+            pltpu.VMEM(phases.shape, F32),
+            pltpu.VMEM(perm.shape, BF16),
+            pltpu.VMEM((2, n, n), F32),
+            pltpu.VMEM((half, n, n), F32),
+            dma((10,)), dma((10,)), dma((9,)),
         ],
         compiler_params=pltpu.CompilerParams(collective_id=0, has_side_effects=True),
         name="halo_in",
@@ -228,13 +246,13 @@
     n = done.shape[-1]
     tall = n + 16
     rows_all = pad_ref.shape[1]
-    slots = centres.shape[3]
+    slots = centres.shape[2]
 
     def place(k):
         at = jnp.where(k < half, (1 - d) * half + k, d * half + k - half)
         batch, slot = at // slots, lax.rem(at, slots)
-        row = centres[0, 0, batch, slot, 0] + halo * (r - 1)
-        col = centres[0, 0, batch, slot, 1]
+        row = centres[0, 0, slot, 0, batch] + halo * (r - 1)
+        col = centres[0, 0, slot, 1, batch]
         base = pl.multiple_of(jnp.minimum(row // 16 * 16, rows_all - tall), 16)
         lane = pl.multiple_of(col // LANE * LANE, LANE)
         return base, lane, row - base, col - lane, slot < occupied[0, 0, batch]
@@ -268,7 +286,7 @@
 
 
 def extract(centres, occupied, padded, n):
-    count = occupied.shape[2] * centres.shape[3]
+    count = occupied.shape[2] * centres.shape[2]
     half = count // 2
     shape = jax.ShapeDtypeStruct((half, 2, n, n), BF16)
     smem = pl.BlockSpec(memory_space=pltpu.SMEM)
@@ -297,12 +315,15 @@
 
 
 def wave_kernel(
-    half, probe_ref, kern, mats_ref, mine_ref, theirs_ref, frames_ref,
+    half, probe_hbm, kern_hbm, mats_hbm, mine_ref, theirs_ref, frames_ref,
     terms_ref, keep_ref, given_ref,
-    windows, frames, grads, total, give, own_sem, frame_sem, swap_send, swap_recv, term_send, term_recv, term_own, give_send, give_recv,
+    windows, frames, probe_ref, kern, mats_ref, fixed, grads, total, give, own_sem, frame_sem, swap_send, swap_recv, term_send, term_recv, term_own, give_send, give_recv,
 ):
     d, r, c = axis_ids()
     n = probe_ref.shape[1]
+    steady = [pltpu.make_async_copy(a, b, fixed.at[i]) for i, (a, b) in enumerate([(mats_hbm, mats_ref), (probe_hbm, probe_ref), (kern_hbm, kern)])]
+    for copy in steady:
+        copy.start()
     partner = (1 - d, r, c)
 
     def own_copy(k):
@@ -334,36 +355,45 @@
 
     total[...] = jnp.zeros_like(total)
     forward, inverse = make_transforms(mats_ref)
-
-    @pl.loop(0, half)
-    def _(k):
-        def window(s):
+    for copy in steady:
+        copy.wait()
+
+    group = 2
+
+    @pl.loop(0, half // group)
+    def _(step):
+        ks = [step * group + i for i in range(group)]
+
+        def window(s, k):
             return [windows[s, k, p].astype(F32) for p in range(2)]
 
-        own_copy(k).wait()
-        frame_copy(k).wait()
-        window_copy(k).wait()
-        fr, fi = forward(*cmul(probe_ref[0], probe_ref[1], *window(0)))
-        pr, pi = inverse(*cmul(fr, fi, kern[0], kern[1]))
-        pr, pi = rounded(pr), rounded(pi)
-        w1r, w1i = window(1)
-        fr, fi = forward(*cmul(pr, pi, w1r, w1i))
-        misfit = fr * fr + fi * fi - frames[k]
-        xr, xi = inverse(misfit * fr, misfit * fi)
-        gr, gi = conj_mul(pr, pi, xr, xi)
-        grads[1, k, 0] = gr.astype(BF16)
-        grads[1, k, 1] = gi.astype(BF16)
-        fr, fi = forward(*conj_mul(w1r, w1i, xr, xi))
-        xr, xi = inverse(*conj_mul(kern[0], kern[1], fr, fi))
-        xr, xi = rounded(xr), rounded(xi)
-        gr, gi = conj_mul(probe_ref[0], probe_ref[1], xr, xi)
-        grads[0, k, 0] = gr.astype(BF16)
-        grads[0, k, 1] = gi.astype(BF16)
-        lr, li = conj_mul(*window(0), xr, xi)
-        total[0] += lr
-        total[1] += li
-        for copy in term_copies(k):
-            copy.start()
+        for k in ks:
+            own_copy(k).wait()
+            frame_copy(k).wait()
+            window_copy(k).wait()
+        waves = forward([cmul(probe_ref[0], probe_ref[1], *window(0, k)) for k in ks])
+        waves = inverse([cmul(fr, fi, kern[0], kern[1]) for fr, fi in waves])
+        waves = [(rounded(pr), rounded(pi)) for pr, pi in waves]
+        fields = forward([cmul(*wave, *window(1, k)) for wave, k in zip(waves, ks)])
+        misfits = [fr * fr + fi * fi - frames[k] for (fr, fi), k in zip(fields, ks)]
+        fields = inverse([(m * fr, m * fi) for (fr, fi), m in zip(fields, misfits)])
+        for k, wave, field in zip(ks, waves, fields):
+            gr, gi = conj_mul(*wave, *field)
+            grads[1, k, 0] = gr.astype(BF16)
+            grads[1, k, 1] = gi.astype(BF16)
+        fields = forward([conj_mul(*window(1, k), *field) for k, field in zip(ks, fields)])
+        fields = inverse([conj_mul(kern[0], kern[1], *field) for field in fields])
+        fields = [(rounded(xr), rounded(xi)) for xr, xi in fields]
+        for k, field in zip(ks, fields):
+            gr, gi = conj_mul(probe_ref[0], probe_ref[1], *field)
+            grads[0, k, 0] = gr.astype(BF16)
+            grads[0, k, 1] = gi.astype(BF16)
+            lr, li = conj_mul(*window(0, k), *field)
+            total[0] += lr
+            total[1] += li
+        for k in ks:
+            for copy in term_copies(k):
+                copy.start()
 
     mid = n // 2
     for p in range(2):
@@ -391,11 +421,15 @@
             jax.ShapeDtypeStruct((2, n // 2, n), F32),
             jax.ShapeDtypeStruct((2, n // 2, n), BF16),
         ),
-        in_specs=[vmem, vmem, vmem, ANY, ANY, ANY],
+        in_specs=[ANY] * 6,
         out_specs=(ANY, vmem, ANY),
         scratch_shapes=[
             pltpu.VMEM((2, half, 2, n, n), BF16),
             pltpu.VMEM((half, n, n), F32),
+            pltpu.VMEM(probe.shape, F32),
+            pltpu.VMEM(kern.shape, F32),
+            pltpu.VMEM(mats.shape, BF16),
+            dma((3,)),
             pltpu.VMEM((2, half, 2, n, n), BF16),
             pltpu.VMEM((2, n, n), F32),
             pltpu.VMEM((2, n // 2, n), BF16),
@@ -406,58 +440,64 @@
     )(probe, kern, mats, mine, theirs, frames)
 
 
-def scatter_kernel(halo, centres, terms_ref, centre_ref, row_ref, side_ref, corner_ref, terms, acc, load, store):
+def scatter_kernel(halo, centres, terms_ref, centre_ref, row_ref, side_ref, corner_ref, terms, acc, row_buf, side_buf, corner_buf, load, store):
     _, r, _ = axis_ids()
     count, _, n, _ = terms.shape
     _, _, rows, cols = centre_ref.shape
-    slots = centres.shape[3]
-
-    def term_load(k):
-        return pltpu.make_async_copy(terms_ref.at[k], terms.at[k], load.at[k])
-
-    for k in range(count):
-        term_load(k).start()
-    acc[...] = jnp.zeros_like(acc)
-
-    @pl.loop(0, count)
-    def _(k):
-        term_load(k).wait()
-        row = centres[0, 0, k // slots, lax.rem(k, slots), 0] + halo * (r - 1)
-        col = centres[0, 0, k // slots, lax.rem(k, slots), 1]
-        top = pl.multiple_of(row // 8 * 8, 8)
-        lane = pl.multiple_of(col // LANE * LANE, LANE)
-        for p in range(2):
-            acc[p, pl.ds(top, n + 8), pl.ds(lane, n + LANE)] += shifted_out(terms[k, p].astype(F32), row - top, col - lane)
-
+    slots = centres.shape[2]
+
+    def term_load(p, k):
+        return pltpu.make_async_copy(terms_ref.at[k, p], terms.at[k, p], load.at[p, k])
+
+    for p in range(2):
+        for k in range(count):
+            term_load(p, k).start()
     mine = pl.ds(pl.multiple_of(halo * r, halo), rows)
     far = pl.ds(pl.multiple_of(rows * (1 - r), halo), halo)
-    stores = [pltpu.make_async_copy(acc.at[p, mine, pl.ds(halo, cols)], centre_ref.at[p, 0], store.at[p]) for p in range(2)]
-    for copy in stores:
-        copy.start()
+    stores = []
+
+    def put(src, dst):
+        stores.append(pltpu.make_async_copy(src, dst, store.at[len(stores)]))
+        stores[-1].start()
+
     for p in range(2):
-        row_ref[p] = acc[p, far, pl.ds(halo, cols)].astype(BF16)
+        acc[p] = jnp.zeros(acc.shape[1:], F32)
+
+        @pl.loop(0, count)
+        def _(k):
+            term_load(p, k).wait()
+            row = centres[0, 0, lax.rem(k, slots), 0, k // slots] + halo * (r - 1)
+            col = centres[0, 0, lax.rem(k, slots), 1, k // slots]
+            top = pl.multiple_of(row // 8 * 8, 8)
+            lane = pl.multiple_of(col // LANE * LANE, LANE)
+            acc[p, pl.ds(top, n + 8), pl.ds(lane, n + LANE)] += shifted_out(terms[k, p].astype(F32), row - top, col - lane)
+
+        put(acc.at[p, mine, pl.ds(halo, cols)], centre_ref.at[p, 0])
+        row_buf[p] = acc[p, far, pl.ds(halo, cols)].astype(BF16)
+        put(row_buf.at[p], row_ref.at[p])
         for i, at in enumerate((halo + cols, 0)):
-            side_ref[i, p] = acc[p, mine, pl.ds(at, halo)].astype(BF16)
-            corner_ref[i, p] = acc[p, far, pl.ds(at, halo)].astype(BF16)
+            side_buf[i, p] = acc[p, mine, pl.ds(at, halo)].astype(BF16)
+            put(side_buf.at[i, p], side_ref.at[i, p])
+            corner_buf[i, p] = acc[p, far, pl.ds(at, halo)].astype(BF16)
+            put(corner_buf.at[i, p], corner_ref.at[i, p])
     for copy in stores:
         copy.wait()
 
 
 def scatter(centres, terms, rows, cols, halo):
     count, _, n, _ = terms.shape
-    vmem = pl.BlockSpec(memory_space=pltpu.VMEM)
     shapes = [((2, 1, rows, cols), F32), ((2, halo, cols), BF16), ((2, 2, rows, halo), BF16), ((2, 2, halo, halo), BF16)]
     return pl.pallas_call(
         functools.partial(scatter_kernel, halo),
         out_shape=tuple(jax.ShapeDtypeStruct(s, t) for s, t in shapes),
         in_specs=[pl.BlockSpec(memory_space=pltpu.SMEM), ANY],
-        out_specs=(ANY, vmem, vmem, vmem),
+        out_specs=(ANY,) * 4,
         scratch_shapes=[
             pltpu.VMEM(terms.shape, BF16),
             pltpu.VMEM((2, rows + halo + 8, cols + 2 * halo), F32),
-            pltpu.SemaphoreType.DMA((count,)),
-            pltpu.SemaphoreType.DMA((2,)),
-        ],
+        ]
+        + [pltpu.VMEM(s, t) for s, t in shapes[1:]]
+        + [pltpu.SemaphoreType.DMA((2, count)), pltpu.SemaphoreType.DMA((12,))],
         name="scatter",
     )(centres, terms)
 
@@ -472,7 +512,7 @@
     return (d, r, q * 2 + lax.rem(c, 2))
 
 
-def return_kernel(row_ref, side_ref, corner_ref, keep_ref, got_ref, row_out, side_out, corner_out, probe_out, buf, line, plane, strips, xs, ps, gs):
+def return_kernel(row_ref, side_ref, corner_ref, keep_hbm, got_hbm, row_out, side_out, corner_out, probe_out, keep_ref, got_ref, buf, line, plane, final, local, strips, xs, ps, gs):
     d, r, c = axis_ids()
     planes = lax.axis_size("col") // 2
     my_x = r * 2 + lax.rem(c, 2)
@@ -480,6 +520,9 @@
     peers = neighbours()
     line_peers = [lax.rem(my_x + t, 4) for t in range(1, 4)]
     plane_peers = [lax.rem(my_p + t, planes) for t in range(1, planes)]
+    loads = [pltpu.make_async_copy(a, b, local.at[i]) for i, (a, b) in enumerate([(keep_hbm, keep_ref), (got_hbm, got_ref)])]
+    for load in loads:
+        load.start()
     meet(peers + [x_peer(q) for q in line_peers] + [plane_peer(q) for q in plane_peers])
     wide = row_ref.shape[-1] // 2
     groups = [[] for _ in range(4)]
@@ -496,6 +539,8 @@
             copies.append(remote(s, t, strips, len(copies), peer))
             copies[-1].start()
 
+    for load in loads:
+        load.wait()
     half_rows, n = keep_ref.shape[1:]
     at = 0
     for p in range(2):
@@ -533,12 +578,15 @@
     launch(ORDER[2])
     for q in line_peers:
         receive(line.at[q], xs, q, x_peer(q))
-    probe_out[pl.ds(my_p * share, share)] = (line[0] + line[1]) + (line[2] + line[3])
+    final[...] = (line[0] + line[1]) + (line[2] + line[3])
+    own = pltpu.make_async_copy(final, piece(probe_out, my_p), local.at[2])
+    own.start()
     for q in plane_peers:
-        send(piece(probe_out, my_p), piece(probe_out, my_p), gs, q, my_p, plane_peer(q))
+        send(final, piece(probe_out, my_p), gs, q, my_p, plane_peer(q))
     launch(ORDER[3])
     for q in plane_peers:
         receive(piece(probe_out, q), gs, q, plane_peer(q))
+    own.wait()
     for copy in sent:
         copy.wait_send()
     for copy in copies:
@@ -549,17 +597,20 @@
     chunks = keep.size // (8 * LANE)
     planes = lax.axis_size("col") // 2
     share = chunks // planes
-    vmem = pl.BlockSpec(memory_space=pltpu.VMEM)
     dma = lambda n: [pltpu.SemaphoreType.DMA((n,)), pltpu.SemaphoreType.DMA((n,))]
     return pl.pallas_call(
         return_kernel_flat,
         out_shape=tuple(jax.ShapeDtypeStruct(a.shape, a.dtype) for a in (row, side, corner)) + (jax.ShapeDtypeStruct((chunks, 8, LANE), F32),),
-        in_specs=[ANY, ANY, ANY, vmem, vmem],
-        out_specs=(ANY, ANY, ANY, vmem),
+        in_specs=[ANY] * 5,
+        out_specs=(ANY,) * 4,
         scratch_shapes=[
+            pltpu.VMEM(keep.shape, F32),
+            pltpu.VMEM(got.shape, BF16),
             pltpu.VMEM((chunks, 8, LANE), F32),
             pltpu.VMEM((4, share, 8, LANE), F32),
             pltpu.VMEM((planes, share, 8, LANE), F32),
+            pltpu.VMEM((share, 8, LANE), F32),
+            pltpu.SemaphoreType.DMA((3,)),
         ]
         + dma(12) + dma(4) + dma(planes) + dma(planes),
         compiler_params=pltpu.CompilerParams(collective_id=3, has_side_effects=True),
@@ -568,31 +619,34 @@
 
 
 def return_kernel_flat(*refs):
-    sems = refs[12:]
-    return_kernel(*refs[:12], *[sems[i : i + 2] for i in range(0, 8, 2)])
-
-
-def fold_kernel(halo, centre_ref, row_ref, side_ref, corner_ref, chunks_ref, out_ref, probe_ref, sides, middle, load, store):
+    sems = refs[16:]
+    return_kernel(*refs[:16], *[sems[i : i + 2] for i in range(0, 8, 2)])
+
+
+def fold_kernel(halo, centre_ref, row_hbm, side_hbm, corner_hbm, chunks_hbm, out_ref, probe_out, sides, middle, row_ref, side_ref, corner_ref, chunks_ref, probe_ref, load, extra, store):
     _, r, _ = axis_ids()
     _, _, rows, cols = out_ref.shape
     edge = pl.ds(pl.multiple_of((rows - halo) * (1 - r), halo), halo)
     inner = pl.ds(halo, cols - 2 * halo)
+    strips = [(row_hbm, row_ref), (side_hbm, side_ref), (corner_hbm, corner_ref), (chunks_hbm, chunks_ref)]
     places = []
     for p in range(2):
         places.append((out_ref.at[p, 0, edge, inner], middle.at[p]))
         for i in range(2):
             places.append((out_ref.at[p, 0, :, pl.ds(i * (cols - halo), halo)], sides.at[i, p]))
+    brought = [pltpu.make_async_copy(a, b, extra.at[j]) for j, (a, b) in enumerate(strips)]
     loads = [pltpu.make_async_copy(a, b, load.at[j]) for j, (a, b) in enumerate(places)]
     stores = [pltpu.make_async_copy(b, a, store.at[j]) for j, (a, b) in enumerate(places)]
-    for copy in loads:
+    stores.append(pltpu.make_async_copy(probe_ref, probe_out, store.at[len(places)]))
+    brought[0].start()
+    loads[0].start()
+    brought[1].start()
+    brought[2].start()
+    for copy in loads[1:]:
         copy.start()
-    at = 0
-    _, half_rows, n = probe_ref.shape
-    for p in range(2):
-        for t in range(half_rows // 8):
-            for h in range(n // LANE):
-                probe_ref[p, pl.ds(8 * t, 8), pl.ds(LANE * h, LANE)] = chunks_ref[at]
-                at += 1
+    brought[3].start()
+    for copy in brought[:3]:
+        copy.wait()
     for p in range(2):
         loads[3 * p].wait()
         middle[p] += row_ref[p, :, inner].astype(F32)
@@ -602,6 +656,15 @@
             sides[i, p] += side_ref[i, p].astype(F32)
             sides[i, p, edge, :] += row_ref[p, :, pl.ds(i * (cols - halo), halo)].astype(F32) + corner_ref[i, p].astype(F32)
             stores[3 * p + 1 + i].start()
+    brought[3].wait()
+    at = 0
+    _, half_rows, n = probe_ref.shape
+    for p in range(2):
+        for t in range(half_rows // 8):
+            for h in range(n // LANE):
+                probe_ref[p, pl.ds(8 * t, 8), pl.ds(LANE * h, LANE)] = chunks_ref[at]
+                at += 1
+    stores[-1].start()
     for copy in stores:
         copy.wait()
 
@@ -609,18 +672,18 @@
 def fold(centre, row, side, corner, chunks, n):
     halo = row.shape[1]
     _, _, rows, cols = centre.shape
-    vmem = pl.BlockSpec(memory_space=pltpu.VMEM)
     return pl.pallas_call(
         functools.partial(fold_kernel, halo),
         out_shape=(jax.ShapeDtypeStruct(centre.shape, F32), jax.ShapeDtypeStruct((2, n // 2, n), F32)),
-        in_specs=[ANY, vmem, vmem, vmem, vmem],
-        out_specs=(ANY, vmem),
+        in_specs=[ANY] * 5,
+        out_specs=(ANY, ANY),
         scratch_shapes=[
             pltpu.VMEM((2, 2, rows, halo), F32),
             pltpu.VMEM((2, halo, cols - 2 * halo), F32),
-            pltpu.SemaphoreType.DMA((6,)),
-            pltpu.SemaphoreType.DMA((6,)),
-        ],
+        ]
+        + [pltpu.VMEM(a.shape, a.dtype) for a in (row, side, corner, chunks)]
+        + [pltpu.VMEM((2, n // 2, n), F32)]
+        + [pltpu.SemaphoreType.DMA((6,)), pltpu.SemaphoreType.DMA((4,)), pltpu.SemaphoreType.DMA((7,))],
         input_output_aliases={0: 0},
         name="fold",
     )(centre, row, side, corner, chunks)
@@ -630,6 +693,7 @@
     n = probe.shape[1]
     _, rows, cols = object_re.shape
     mats, perm = (jnp.asarray(x) for x in constants(n))
+    centres = jnp.transpose(centres, (0, 1, 3, 4, 2))
     padded, kern, frames = exchange_halo(object_re, object_im, phases, perm, measured, n // 2)
     mine, theirs = extract(centres, occupied, padded, n)
     terms, keep, given = waves(probe, kern, mats, mine, theirs, frames)

time: 110 us -> 96.5 us (0.88)
  Pallas kernels: 107 us -> 95.2 us
  local copies, waits for them, and re-layouts: 1.36 us -> 0 us
    pallas_call x1, Pallas kernels: 23.5 us -> 16.4 us  [waves(): pl.pallas_call(functools.partial(wave_kernel, half), out_shape=(jax.Shape...]
    pallas_call x1, Pallas kernels: 34 us -> 31.9 us  [exchange_halo(): pl.pallas_call(functools.partial(halo_kernel, half, halo), out_shape=(jax...]
    pallas_call x1, Pallas kernels: 34.6 us -> 33.1 us  [send_back(): pl.pallas_call(return_kernel_flat, out_shape=tuple((jax.ShapeDtypeStruct(...]
    unnamed x1 -> x0, local copies, waits for them, and re-layouts: 1.36 us -> none
    pallas_call x1, Pallas kernels: 4.38 us -> 3.12 us  [fold(): pl.pallas_call(functools.partial(fold_kernel, halo), out_shape=(jax.Shape...]
where the time goes in v3:
time: 96.5 us; the launch traced here: 95.9 us
  Pallas kernels  95.2 us (99%)
    pallas_call x1, Pallas kernels, send_back(): pl.pallas_call(return_kernel_flat, out_shape=tuple((jax.ShapeDtypeStruct(...  33.1 us
    pallas_call x1, Pallas kernels, exchange_halo(): pl.pallas_call(functools.partial(halo_kernel, half, halo), out_shape=(jax...  31.9 us
    pallas_call x1, Pallas kernels, waves(): pl.pallas_call(functools.partial(wave_kernel, half), out_shape=(jax.Shape...  16.4 us
    pallas_call x1, Pallas kernels, scatter(): pl.pallas_call(functools.partial(scatter_kernel, halo), out_shape=tuple((...  6.11 us
    pallas_call x1, Pallas kernels, extract(): pl.pallas_call(functools.partial(extract_kernel, n // 2), out_shape=(shap...  4.63 us
    pallas_call x1, Pallas kernels, fold(): pl.pallas_call(functools.partial(fold_kernel, halo), out_shape=(jax.Shape...  3.12 us

profile of v3, /device:TPU:0, one launch (start us, length us, event | category | flops | bytes accessed | tf_op | source)
XLA Modules:
  0.0 95.9 jit_solution(8782677121317304097)
XLA Ops:
  0.6 31.9 %halo_in.1 = (bf16[2,640,1280]{2,1,0:T(8,128)(2,1)}, f32[2,256,256]{2,1,0:T(8,128)}, f32[4,256,256]{2,1,0:T(8,128)}) custom-call(f32[256,256]{1,0:T(8,128)} %phases_ref.1, bf16[2,256,256]{2,1,0:T(8,128)(2,1)} %constant.5.clone.perm_ref, bf16[1,512,1024]{2,1,0:T(8,128)(2,1)} %re_ref.1, bf16[1,512,1024]{2,1,0:T(8,128)(2,1)} %im_ref.1, ...), custom_call_target="tpu_custom_call" | custom-call | tf_op jit(solution)/shard_map/halo_in/pallas_call | solution.py:219
  32.6 4.6 %extract.1 = (bf16[4,2,256,256]{3,2,1,0:T(8,128)(2,1)}, bf16[4,2,256,256]{3,2,1,0:T(8,128)(2,1)}) custom-call(s32[1,1,2,2,4]{4,3,2,1,0:T(2,128)} %bitcast.1, s32[1,1,4]{2,1,0:T(1,128)} %occupied.1, bf16[2,640,1280]{2,1,0:T(8,128)(2,1)} %get-tuple-element.19.pad_ref), custom_call_target="tpu_custom_call" | custom-call | tf_op jit(solution)/shard_map/extract/pallas_call | solution.py:293
  37.2 16.4 %waves.1 = (bf16[8,2,256,256]{3,2,1,0:T(8,128)(2,1)}, f32[2,128,256]{2,1,0:T(8,128)}, bf16[2,128,256]{2,1,0:T(8,128)(2,1)}) custom-call(f32[2,256,256]{2,1,0:T(8,128)} %probe_hbm.1, f32[2,256,256]{2,1,0:T(8,128)} %get-tuple-element.18.kern_hbm, bf16[8,256,256]{2,1,0:T(8,128)(2,1)} %constant.4.clone.mats_hbm, ...), custom_call_target="tpu_custom_call" | custom-call | tf_op jit(solution)/shard_map/waves/pallas_call | solution.py:417
  53.6 6.1 %scatter.1 = (f32[2,1,512,1024]{3,2,1,0:T(8,128)}, bf16[2,128,1024]{2,1,0:T(8,128)(2,1)}, bf16[2,2,512,128]{3,2,1,0:T(8,128)(2,1)}, bf16[2,2,128,128]{3,2,1,0:T(8,128)(2,1)}) custom-call(s32[1,1,2,2,4]{4,3,2,1,0:T(2,128)} %bitcast.2, bf16[8,2,256,256]{3,2,1,0:T(8,128)(2,1)} %get-tuple-element.23.terms_ref), custom_call_target="tpu_custom_call" | custom-call | tf_op jit(solution)/shard_map/scatter/pallas_call | solution.py:490
  59.7 33.1 %halo_out.1 = (bf16[2,128,1024]{2,1,0:T(8,128)(2,1)}, bf16[2,2,512,128]{3,2,1,0:T(8,128)(2,1)}, bf16[2,2,128,128]{3,2,1,0:T(8,128)(2,1)}, f32[64,8,128]{2,1,0:T(8,128)}) custom-call(bf16[2,128,1024]{2,1,0:T(8,128)(2,1)} %get-tuple-element.25.refs_0_, bf16[2,2,512,128]{3,2,1,0:T(8,128)(2,1)} %get-tuple-element.26.refs_1_, ...), custom_call_target="tpu_custom_call" | custom-call | tf_op jit(solution)/shard_map/halo_out/pallas_call | solution.py:601
  92.8 3.1 %fold.1 = (f32[2,1,512,1024]{3,2,1,0:T(8,128)}, f32[2,128,256]{2,1,0:T(8,128)}) custom-call(f32[2,1,512,1024]{3,2,1,0:T(8,128)} %get-tuple-element.24.centre_ref, bf16[2,128,1024]{2,1,0:T(8,128)(2,1)} %get-tuple-element.30.row_hbm, bf16[2,2,512,128]{3,2,1,0:T(8,128)(2,1)} %get-tuple-element.31.side_hbm, ...), custom_call_target="tpu_custom_call", output_to_operand_aliasing={{0}: (0, {})} | custom-call | tf_op jit(solution)/shard_map/fold/pallas_call | solution.py:675

commit v4 on v3

--- a/solution.py
+++ b/solution.py
@@ -13,7 +13,7 @@
 BF16 = jnp.bfloat16
 ANY = pl.BlockSpec(memory_space=pl.ANY)
 LANE = 128
-ORDER = ((), (0, 1), (2,), (3,))
+ORDER = ((0,), (1,), (2,), (3,))
 REDUCE = True
 NAME = 'halo_out'
 
@@ -89,27 +89,30 @@
     return high, (x - high.astype(F32)).astype(BF16)
 
 
-def product(a, b, passes):
-    (ah, al), (bh, bl) = a, b
-    if passes == 3:
-        lhs, rhs = [ah, ah, al], [bh, bl, bh]
-    else:
-        lhs, rhs = [ah], [bh]
-    lhs = jnp.concatenate(lhs, 1) if len(lhs) > 1 else lhs[0]
-    rhs = jnp.concatenate(rhs, 0) if len(rhs) > 1 else rhs[0]
-    return jnp.dot(lhs, rhs, preferred_element_type=F32)
-
-
 def make_transforms(mats_ref):
     def mat(parity, transposed):
         at = parity * 4 + transposed * 2
         return mats_ref[at], mats_ref[at + 1]
 
-    def left(z, parity, transposed):
-        return product(mat(parity, transposed), split(jnp.concatenate(z, 0)), 3)
-
-    def right(z, parity, transposed):
-        return product(split(jnp.concatenate(z, 1)), mat(parity, transposed), 3)
+    def left(z, parity, transposed, exact):
+        high, low = mat(parity, transposed)
+        zh, zl = split(jnp.concatenate(z, 0))
+        if not exact:
+            return jnp.dot(jnp.concatenate([high, high], 1), jnp.concatenate([zh, zl], 0), preferred_element_type=F32)
+        out = jnp.dot(jnp.concatenate([high, low], 0), zh, preferred_element_type=F32)
+        n = out.shape[0] // 2
+        return out[:n] + (out[n:] + jnp.dot(high, zl, preferred_element_type=F32))
+
+    def right(z, parity, transposed, exact):
+        high, low = mat(parity, transposed)
+        zh, zl = split(jnp.concatenate(z, 1))
+        if not exact:
+            out = jnp.dot(jnp.concatenate([zh, zl], 0), high, preferred_element_type=F32)
+            n = out.shape[0] // 2
+            return out[:n] + out[n:]
+        out = jnp.dot(jnp.concatenate([zh, zl], 0), high, preferred_element_type=F32)
+        n = out.shape[0] // 2
+        return out[:n] + (out[n:] + jnp.dot(zh, low, preferred_element_type=F32))
 
     def halves(z):
         h = z.shape[0] // 2
@@ -122,16 +125,16 @@
     def fold(parts, parity):
         return parts[0] + parts[1] if parity == 0 else parts[0] - parts[1]
 
-    def forward(fields):
-        outs = [[left([fold(halves(x), parity) for x in z], parity, 0) for parity in range(2)] for z in fields]
+    def forward(fields, exact=True):
+        outs = [[left([fold(halves(x), parity) for x in z], parity, 0, exact) for parity in range(2)] for z in fields]
         fields = [[jnp.concatenate([halves(o)[i] for o in out], 0) for i in range(2)] for out in outs]
-        outs = [[right([fold(sides(x), parity) for x in z], parity, 1) for parity in range(2)] for z in fields]
+        outs = [[right([fold(sides(x), parity) for x in z], parity, 1, exact) for parity in range(2)] for z in fields]
         return [[jnp.concatenate([sides(o)[i] for o in out], 1) for i in range(2)] for out in outs]
 
-    def inverse(fields):
-        outs = [[left([halves(x)[parity] for x in z], parity, 1) for parity in range(2)] for z in fields]
+    def inverse(fields, exact=True):
+        outs = [[left([halves(x)[parity] for x in z], parity, 1, exact) for parity in range(2)] for z in fields]
         fields = [[jnp.concatenate([fold([halves(o)[i] for o in out], q) for q in range(2)], 0) for i in range(2)] for out in outs]
-        outs = [[right([sides(x)[parity] for x in z], parity, 0) for parity in range(2)] for z in fields]
+        outs = [[right([sides(x)[parity] for x in z], parity, 0, exact) for parity in range(2)] for z in fields]
         return [[jnp.concatenate([fold([sides(o)[i] for o in out], q) for q in range(2)], 1) for i in range(2)] for out in outs]
 
     return forward, inverse
@@ -316,8 +319,8 @@
 
 def wave_kernel(
     half, probe_hbm, kern_hbm, mats_hbm, mine_ref, theirs_ref, frames_ref,
-    terms_ref, keep_ref, given_ref,
-    windows, frames, probe_ref, kern, mats_ref, fixed, grads, total, give, own_sem, frame_sem, swap_send, swap_recv, term_send, term_recv, term_own, give_send, give_recv,
+    terms_ref, total_ref,
+    windows, frames, probe_ref, kern, mats_ref, fixed, grads, total, own_sem, frame_sem, swap_send, swap_recv, term_send, term_recv, term_own, total_sem,
 ):
     d, r, c = axis_ids()
     n = probe_ref.shape[1]
@@ -345,13 +348,13 @@
     @pl.loop(0, half)
     def _(k):
         own_copy(k).start()
-        frame_copy(k).start()
 
     meet([partner])
 
     @pl.loop(0, half)
     def _(k):
         window_copy(k).start()
+        frame_copy(k).start()
 
     total[...] = jnp.zeros_like(total)
     forward, inverse = make_transforms(mats_ref)
@@ -376,13 +379,13 @@
         waves = [(rounded(pr), rounded(pi)) for pr, pi in waves]
         fields = forward([cmul(*wave, *window(1, k)) for wave, k in zip(waves, ks)])
         misfits = [fr * fr + fi * fi - frames[k] for (fr, fi), k in zip(fields, ks)]
-        fields = inverse([(m * fr, m * fi) for (fr, fi), m in zip(fields, misfits)])
+        fields = inverse([(m * fr, m * fi) for (fr, fi), m in zip(fields, misfits)], False)
         for k, wave, field in zip(ks, waves, fields):
             gr, gi = conj_mul(*wave, *field)
             grads[1, k, 0] = gr.astype(BF16)
             grads[1, k, 1] = gi.astype(BF16)
-        fields = forward([conj_mul(*window(1, k), *field) for k, field in zip(ks, fields)])
-        fields = inverse([conj_mul(kern[0], kern[1], *field) for field in fields])
+        fields = forward([conj_mul(*window(1, k), *field) for k, field in zip(ks, fields)], False)
+        fields = inverse([conj_mul(kern[0], kern[1], *field) for field in fields], False)
         fields = [(rounded(xr), rounded(xi)) for xr, xi in fields]
         for k, field in zip(ks, fields):
             gr, gi = conj_mul(probe_ref[0], probe_ref[1], *field)
@@ -391,15 +394,10 @@
             lr, li = conj_mul(*window(0, k), *field)
             total[0] += lr
             total[1] += li
-        for k in ks:
             for copy in term_copies(k):
                 copy.start()
 
-    mid = n // 2
-    for p in range(2):
-        give[p] = total[p, pl.ds(pl.multiple_of((1 - d) * mid, 8), mid), :].astype(BF16)
-        keep_ref[p] = total[p, pl.ds(pl.multiple_of(d * mid, 8), mid), :]
-    last_copy = pltpu.make_async_remote_copy(give, given_ref, give_send, give_recv, device_id=partner, device_id_type=MESH)
+    last_copy = pltpu.make_async_copy(total, total_ref, total_sem)
     last_copy.start()
 
     @pl.loop(0, half)
@@ -412,17 +410,15 @@
 
 def waves(probe, kern, mats, mine, theirs, frames):
     half, _, n, _ = mine.shape
-    vmem = pl.BlockSpec(memory_space=pltpu.VMEM)
     dma = pltpu.SemaphoreType.DMA
     return pl.pallas_call(
         functools.partial(wave_kernel, half),
         out_shape=(
             jax.ShapeDtypeStruct((2 * half, 2, n, n), BF16),
-            jax.ShapeDtypeStruct((2, n // 2, n), F32),
-            jax.ShapeDtypeStruct((2, n // 2, n), BF16),
+            jax.ShapeDtypeStruct((2, n, n), F32),
         ),
         in_specs=[ANY] * 6,
-        out_specs=(ANY, vmem, ANY),
+        out_specs=(ANY, ANY),
         scratch_shapes=[
             pltpu.VMEM((2, half, 2, n, n), BF16),
             pltpu.VMEM((half, n, n), F32),
@@ -432,9 +428,8 @@
             dma((3,)),
             pltpu.VMEM((2, half, 2, n, n), BF16),
             pltpu.VMEM((2, n, n), F32),
-            pltpu.VMEM((2, n // 2, n), BF16),
         ]
-        + [dma((half,))] * 7 + [dma(()), dma(())],
+        + [dma((half,))] * 7 + [dma(())],
         compiler_params=pltpu.CompilerParams(collective_id=1, has_side_effects=True),
         name="waves",
     )(probe, kern, mats, mine, theirs, frames)
@@ -512,7 +507,7 @@
     return (d, r, q * 2 + lax.rem(c, 2))
 
 
-def return_kernel(row_ref, side_ref, corner_ref, keep_hbm, got_hbm, row_out, side_out, corner_out, probe_out, keep_ref, got_ref, buf, line, plane, final, local, strips, xs, ps, gs):
+def return_kernel(row_ref, side_ref, corner_ref, total_ref, row_out, side_out, corner_out, probe_out, keep_ref, got_ref, buf, line, plane, final, local, strips, xs, ps, gs, give):
     d, r, c = axis_ids()
     planes = lax.axis_size("col") // 2
     my_x = r * 2 + lax.rem(c, 2)
@@ -520,10 +515,17 @@
     peers = neighbours()
     line_peers = [lax.rem(my_x + t, 4) for t in range(1, 4)]
     plane_peers = [lax.rem(my_p + t, planes) for t in range(1, planes)]
-    loads = [pltpu.make_async_copy(a, b, local.at[i]) for i, (a, b) in enumerate([(keep_hbm, keep_ref), (got_hbm, got_ref)])]
-    for load in loads:
-        load.start()
-    meet(peers + [x_peer(q) for q in line_peers] + [plane_peer(q) for q in plane_peers])
+    mid = keep_ref.shape[1]
+
+    def rows_of(depth):
+        return total_ref.at[:, pl.ds(pl.multiple_of(depth * mid, 8), mid)]
+
+    load = pltpu.make_async_copy(rows_of(d), keep_ref, local.at[0])
+    load.start()
+    partner = (1 - d, r, c)
+    meet([partner] + peers + [x_peer(q) for q in line_peers] + [plane_peer(q) for q in plane_peers])
+    other = pltpu.make_async_remote_copy(rows_of(1 - d), got_ref, give[0].at[0], give[1].at[0], device_id=partner, device_id_type=MESH)
+    other.start()
     wide = row_ref.shape[-1] // 2
     groups = [[] for _ in range(4)]
     for p in range(2):
@@ -539,15 +541,16 @@
             copies.append(remote(s, t, strips, len(copies), peer))
             copies[-1].start()
 
-    for load in loads:
-        load.wait()
+    launch(ORDER[0])
+    load.wait()
+    other.wait()
     half_rows, n = keep_ref.shape[1:]
     at = 0
     for p in range(2):
         for t in range(half_rows // 8):
             for h in range(n // LANE):
                 place = (p, pl.ds(8 * t, 8), pl.ds(LANE * h, LANE))
-                buf[at] = keep_ref[place] + got_ref[place].astype(F32)
+                buf[at] = keep_ref[place] + got_ref[place]
                 at += 1
     share = at // planes
 
@@ -563,7 +566,6 @@
         pltpu.make_async_remote_copy(dst, dst, sems[0].at[q], sems[1].at[q], device_id=peer, device_id_type=MESH).wait_recv()
 
     sent = []
-    launch(ORDER[0])
     for q in plane_peers:
         send(piece(buf, q), plane.at[my_p], ps, q, my_p, plane_peer(q))
     launch(ORDER[1])
@@ -593,34 +595,35 @@
         copy.wait()
 
 
-def send_back(row, side, corner, keep, got):
-    chunks = keep.size // (8 * LANE)
+def send_back(row, side, corner, total):
+    _, n, _ = total.shape
+    chunks = n * n // (8 * LANE)
     planes = lax.axis_size("col") // 2
     share = chunks // planes
     dma = lambda n: [pltpu.SemaphoreType.DMA((n,)), pltpu.SemaphoreType.DMA((n,))]
     return pl.pallas_call(
         return_kernel_flat,
         out_shape=tuple(jax.ShapeDtypeStruct(a.shape, a.dtype) for a in (row, side, corner)) + (jax.ShapeDtypeStruct((chunks, 8, LANE), F32),),
-        in_specs=[ANY] * 5,
+        in_specs=[ANY] * 4,
         out_specs=(ANY,) * 4,
         scratch_shapes=[
-            pltpu.VMEM(keep.shape, F32),
-            pltpu.VMEM(got.shape, BF16),
+            pltpu.VMEM((2, n // 2, n), F32),
+            pltpu.VMEM((2, n // 2, n), F32),
             pltpu.VMEM((chunks, 8, LANE), F32),
             pltpu.VMEM((4, share, 8, LANE), F32),
             pltpu.VMEM((planes, share, 8, LANE), F32),
             pltpu.VMEM((share, 8, LANE), F32),
             pltpu.SemaphoreType.DMA((3,)),
         ]
-        + dma(12) + dma(4) + dma(planes) + dma(planes),
+        + dma(12) + dma(4) + dma(planes) + dma(planes) + dma(1),
         compiler_params=pltpu.CompilerParams(collective_id=3, has_side_effects=True),
         name=NAME,
-    )(row, side, corner, keep, got)
+    )(row, side, corner, total)
 
 
 def return_kernel_flat(*refs):
-    sems = refs[16:]
-    return_kernel(*refs[:16], *[sems[i : i + 2] for i in range(0, 8, 2)])
+    sems = refs[15:]
+    return_kernel(*refs[:15], *[sems[i : i + 2] for i in range(0, 10, 2)])
 
 
 def fold_kernel(halo, centre_ref, row_hbm, side_hbm, corner_hbm, chunks_hbm, out_ref, probe_out, sides, middle, row_ref, side_ref, corner_ref, chunks_ref, probe_ref, load, extra, store):
@@ -696,9 +699,9 @@
     centres = jnp.transpose(centres, (0, 1, 3, 4, 2))
     padded, kern, frames = exchange_halo(object_re, object_im, phases, perm, measured, n // 2)
     mine, theirs = extract(centres, occupied, padded, n)
-    terms, keep, given = waves(probe, kern, mats, mine, theirs, frames)
+    terms, total = waves(probe, kern, mats, mine, theirs, frames)
     centre, row, side, corner = scatter(centres, terms, rows, cols, n // 2)
-    row, side, corner, chunks = send_back(row, side, corner, keep, given)
+    row, side, corner, chunks = send_back(row, side, corner, total)
     return fold(centre, row, side, corner, chunks, n)
 
 

time: 96.5 us -> 94 us (0.974)
  Pallas kernels: 95.2 us -> 92.7 us
    pallas_call x1, Pallas kernels: 16.4 us -> 13.9 us  [waves(): pl.pallas_call(functools.partial(wave_kernel, half), out_shape=(jax.Shape...]
where the time goes in v4:
time: 94 us; the launch traced here: 93.4 us
  Pallas kernels  92.7 us (99%)
    pallas_call x1, Pallas kernels, send_back(): pl.pallas_call(return_kernel_flat, out_shape=tuple((jax.ShapeDtypeStruct(...  33 us
    pallas_call x1, Pallas kernels, exchange_halo(): pl.pallas_call(functools.partial(halo_kernel, half, halo), out_shape=(jax...  31.9 us
    pallas_call x1, Pallas kernels, waves(): pl.pallas_call(functools.partial(wave_kernel, half), out_shape=(jax.Shape...  13.9 us
    pallas_call x1, Pallas kernels, scatter(): pl.pallas_call(functools.partial(scatter_kernel, halo), out_shape=tuple((...  6.1 us
    pallas_call x1, Pallas kernels, extract(): pl.pallas_call(functools.partial(extract_kernel, n // 2), out_shape=(shap...  4.63 us
    pallas_call x1, Pallas kernels, fold(): pl.pallas_call(functools.partial(fold_kernel, halo), out_shape=(jax.Shape...  3.12 us

profile of v4, /device:TPU:0, one launch (start us, length us, event | category | flops | bytes accessed | tf_op | source)
XLA Modules:
  0.0 93.4 jit_solution(17654746287947320881)
XLA Ops:
  0.6 31.9 %halo_in.1 = (bf16[2,640,1280]{2,1,0:T(8,128)(2,1)}, f32[2,256,256]{2,1,0:T(8,128)}, f32[4,256,256]{2,1,0:T(8,128)}) custom-call(f32[256,256]{1,0:T(8,128)} %phases_ref.1, bf16[2,256,256]{2,1,0:T(8,128)(2,1)} %constant.5.clone.perm_ref, bf16[1,512,1024]{2,1,0:T(8,128)(2,1)} %re_ref.1, bf16[1,512,1024]{2,1,0:T(8,128)(2,1)} %im_ref.1, ...), custom_call_target="tpu_custom_call" | custom-call | tf_op jit(solution)/shard_map/halo_in/pallas_call | solution.py:222
  32.6 4.6 %extract.1 = (bf16[4,2,256,256]{3,2,1,0:T(8,128)(2,1)}, bf16[4,2,256,256]{3,2,1,0:T(8,128)(2,1)}) custom-call(s32[1,1,2,2,4]{4,3,2,1,0:T(2,128)} %bitcast.1, s32[1,1,4]{2,1,0:T(1,128)} %occupied.1, bf16[2,640,1280]{2,1,0:T(8,128)(2,1)} %get-tuple-element.18.pad_ref), custom_call_target="tpu_custom_call" | custom-call | tf_op jit(solution)/shard_map/extract/pallas_call | solution.py:296
  37.2 13.9 %waves.1 = (bf16[8,2,256,256]{3,2,1,0:T(8,128)(2,1)}, f32[2,256,256]{2,1,0:T(8,128)}) custom-call(f32[2,256,256]{2,1,0:T(8,128)} %probe_hbm.1, f32[2,256,256]{2,1,0:T(8,128)} %get-tuple-element.17.kern_hbm, bf16[8,256,256]{2,1,0:T(8,128)(2,1)} %constant.4.clone.mats_hbm, bf16[4,2,256,256]{3,2,1,0:T(8,128)(2,1)} %get-tuple-element.19.mine_ref, ...), custom_call_target="tpu_custom_call" | custom-call | tf_op jit(solution)/shard_map/waves/pallas_call | solution.py:414
  51.1 6.1 %scatter.1 = (f32[2,1,512,1024]{3,2,1,0:T(8,128)}, bf16[2,128,1024]{2,1,0:T(8,128)(2,1)}, bf16[2,2,512,128]{3,2,1,0:T(8,128)(2,1)}, bf16[2,2,128,128]{3,2,1,0:T(8,128)(2,1)}) custom-call(s32[1,1,2,2,4]{4,3,2,1,0:T(2,128)} %bitcast.2, bf16[8,2,256,256]{3,2,1,0:T(8,128)(2,1)} %get-tuple-element.22.terms_ref), custom_call_target="tpu_custom_call" | custom-call | tf_op jit(solution)/shard_map/scatter/pallas_call | solution.py:485
  57.2 33.0 %halo_out.1 = (bf16[2,128,1024]{2,1,0:T(8,128)(2,1)}, bf16[2,2,512,128]{3,2,1,0:T(8,128)(2,1)}, bf16[2,2,128,128]{3,2,1,0:T(8,128)(2,1)}, f32[64,8,128]{2,1,0:T(8,128)}) custom-call(bf16[2,128,1024]{2,1,0:T(8,128)(2,1)} %get-tuple-element.24.refs_0_, bf16[2,2,512,128]{3,2,1,0:T(8,128)(2,1)} %get-tuple-element.25.refs_1_, ...), custom_call_target="tpu_custom_call" | custom-call | tf_op jit(solution)/shard_map/halo_out/pallas_call | solution.py:604
  90.2 3.1 %fold.1 = (f32[2,1,512,1024]{3,2,1,0:T(8,128)}, f32[2,128,256]{2,1,0:T(8,128)}) custom-call(f32[2,1,512,1024]{3,2,1,0:T(8,128)} %get-tuple-element.23.centre_ref, bf16[2,128,1024]{2,1,0:T(8,128)(2,1)} %get-tuple-element.28.row_hbm, bf16[2,2,512,128]{3,2,1,0:T(8,128)(2,1)} %get-tuple-element.29.side_hbm, ...), custom_call_target="tpu_custom_call", output_to_operand_aliasing={{0}: (0, {})} | custom-call | tf_op jit(solution)/shard_map/fold/pallas_call | solution.py:678

commit v5 on v4

--- a/solution.py
+++ b/solution.py
@@ -13,7 +13,7 @@
 BF16 = jnp.bfloat16
 ANY = pl.BlockSpec(memory_space=pl.ANY)
 LANE = 128
-ORDER = ((0,), (1,), (2,), (3,))
+ORDER = ((0,), (1,), (), (2,), (3,), ())
 REDUCE = True
 NAME = 'halo_out'
 
@@ -502,19 +502,25 @@
     return (d, q // 2, c // 2 * 2 + lax.rem(q, 2))
 
 
-def plane_peer(q):
+def y_peer(q):
     d, r, c = axis_ids()
-    return (d, r, q * 2 + lax.rem(c, 2))
-
-
-def return_kernel(row_ref, side_ref, corner_ref, total_ref, row_out, side_out, corner_out, probe_out, keep_ref, got_ref, buf, line, plane, final, local, strips, xs, ps, gs, give):
+    return (d, r, c // 8 * 8 + q * 2 + lax.rem(c, 2))
+
+
+def z_peer(q):
     d, r, c = axis_ids()
-    planes = lax.axis_size("col") // 2
+    return (d, r, q * 8 + lax.rem(c, 8))
+
+
+def return_kernel(row_ref, side_ref, corner_ref, total_ref, row_out, side_out, corner_out, probe_out, keep_ref, got_ref, buf, ys_in, y_sum, zs_in, x_in, z_all, local, strips, ys, zs, xs, zg, yg, give):
+    d, r, c = axis_ids()
     my_x = r * 2 + lax.rem(c, 2)
-    my_p = c // 2
+    my_y, my_z = lax.rem(c // 2, 4), c // 8
     peers = neighbours()
-    line_peers = [lax.rem(my_x + t, 4) for t in range(1, 4)]
-    plane_peers = [lax.rem(my_p + t, planes) for t in range(1, planes)]
+
+    def others(me):
+        return [lax.rem(me + t, 4) for t in range(1, 4)]
+
     mid = keep_ref.shape[1]
 
     def rows_of(depth):
@@ -523,7 +529,7 @@
     load = pltpu.make_async_copy(rows_of(d), keep_ref, local.at[0])
     load.start()
     partner = (1 - d, r, c)
-    meet([partner] + peers + [x_peer(q) for q in line_peers] + [plane_peer(q) for q in plane_peers])
+    meet([partner] + peers + [y_peer(q) for q in others(my_y)] + [z_peer(q) for q in others(my_z)])
     other = pltpu.make_async_remote_copy(rows_of(1 - d), got_ref, give[0].at[0], give[1].at[0], device_id=partner, device_id_type=MESH)
     other.start()
     wide = row_ref.shape[-1] // 2
@@ -552,10 +558,12 @@
                 place = (p, pl.ds(8 * t, 8), pl.ds(LANE * h, LANE))
                 buf[at] = keep_ref[place] + got_ref[place]
                 at += 1
-    share = at // planes
-
-    def piece(ref, q):
-        return ref.at[pl.ds(q * share, share)]
+
+    def quarter(ref, q):
+        size = ref.shape[0] // 4
+        return ref.at[pl.ds(q * size, size)]
+
+    sent = []
 
     def send(src, dst, sems, q, me, peer):
         copy = pltpu.make_async_remote_copy(src, dst, sems[0].at[q], sems[1].at[me], device_id=peer, device_id_type=MESH)
@@ -565,29 +573,40 @@
     def receive(dst, sems, q, peer):
         pltpu.make_async_remote_copy(dst, dst, sems[0].at[q], sems[1].at[q], device_id=peer, device_id_type=MESH).wait_recv()
 
-    sent = []
-    for q in plane_peers:
-        send(piece(buf, q), plane.at[my_p], ps, q, my_p, plane_peer(q))
+    for q in others(my_y):
+        send(quarter(buf, q), ys_in.at[my_y], ys, q, my_y, y_peer(q))
     launch(ORDER[1])
-    for q in plane_peers:
-        receive(plane.at[q], ps, q, plane_peer(q))
-    total = buf[pl.ds(my_p * share, share)]
-    for q in plane_peers:
-        total = total + plane[q]
-    line[my_x] = total
-    for q in line_peers:
-        send(line.at[my_x], line.at[my_x], xs, q, my_x, x_peer(q))
+    part = quarter(buf, my_y)[...]
+    for q in others(my_y):
+        receive(ys_in.at[q], ys, q, y_peer(q))
+        part = part + ys_in[q]
+    y_sum[...] = part
+    for q in others(my_z):
+        send(quarter(y_sum, q), zs_in.at[my_z], zs, q, my_z, z_peer(q))
     launch(ORDER[2])
-    for q in line_peers:
-        receive(line.at[q], xs, q, x_peer(q))
-    final[...] = (line[0] + line[1]) + (line[2] + line[3])
-    own = pltpu.make_async_copy(final, piece(probe_out, my_p), local.at[2])
+    part = quarter(y_sum, my_z)[...]
+    for q in others(my_z):
+        receive(zs_in.at[q], zs, q, z_peer(q))
+        part = part + zs_in[q]
+    x_in[my_x] = part
+    for q in others(my_x):
+        send(x_in.at[my_x], x_in.at[my_x], xs, q, my_x, x_peer(q))
+    launch(ORDER[3])
+    for q in others(my_x):
+        receive(x_in.at[q], xs, q, x_peer(q))
+    z_all[my_z] = (x_in[0] + x_in[1]) + (x_in[2] + x_in[3])
+    for q in others(my_z):
+        send(z_all.at[my_z], z_all.at[my_z], zg, q, my_z, z_peer(q))
+    launch(ORDER[4])
+    for q in others(my_z):
+        receive(z_all.at[q], zg, q, z_peer(q))
+    own = pltpu.make_async_copy(z_all, probe_out.at[my_y], local.at[1])
     own.start()
-    for q in plane_peers:
-        send(final, piece(probe_out, my_p), gs, q, my_p, plane_peer(q))
-    launch(ORDER[3])
-    for q in plane_peers:
-        receive(piece(probe_out, q), gs, q, plane_peer(q))
+    for q in others(my_y):
+        send(z_all, probe_out.at[my_y], yg, q, my_y, y_peer(q))
+    launch(ORDER[5])
+    for q in others(my_y):
+        receive(probe_out.at[q], yg, q, y_peer(q))
     own.wait()
     for copy in sent:
         copy.wait_send()
@@ -597,33 +616,34 @@
 
 def send_back(row, side, corner, total):
     _, n, _ = total.shape
-    chunks = n * n // (8 * LANE)
-    planes = lax.axis_size("col") // 2
-    share = chunks // planes
+    share = n * n // (64 * 8 * LANE)
     dma = lambda n: [pltpu.SemaphoreType.DMA((n,)), pltpu.SemaphoreType.DMA((n,))]
+    chunk = lambda *lead: pltpu.VMEM(lead + (8, LANE), F32)
     return pl.pallas_call(
         return_kernel_flat,
-        out_shape=tuple(jax.ShapeDtypeStruct(a.shape, a.dtype) for a in (row, side, corner)) + (jax.ShapeDtypeStruct((chunks, 8, LANE), F32),),
+        out_shape=tuple(jax.ShapeDtypeStruct(a.shape, a.dtype) for a in (row, side, corner)) + (jax.ShapeDtypeStruct((4, 4, 4 * share, 8, LANE), F32),),
         in_specs=[ANY] * 4,
         out_specs=(ANY,) * 4,
         scratch_shapes=[
             pltpu.VMEM((2, n // 2, n), F32),
             pltpu.VMEM((2, n // 2, n), F32),
-            pltpu.VMEM((chunks, 8, LANE), F32),
-            pltpu.VMEM((4, share, 8, LANE), F32),
-            pltpu.VMEM((planes, share, 8, LANE), F32),
-            pltpu.VMEM((share, 8, LANE), F32),
-            pltpu.SemaphoreType.DMA((3,)),
+            chunk(64 * share),
+            chunk(4, 16 * share),
+            chunk(16 * share),
+            chunk(4, 4 * share),
+            chunk(4, 4 * share),
+            chunk(4, 4 * share),
+            pltpu.SemaphoreType.DMA((2,)),
         ]
-        + dma(12) + dma(4) + dma(planes) + dma(planes) + dma(1),
+        + dma(12) + dma(4) * 5 + dma(1),
         compiler_params=pltpu.CompilerParams(collective_id=3, has_side_effects=True),
         name=NAME,
     )(row, side, corner, total)
 
 
 def return_kernel_flat(*refs):
-    sems = refs[15:]
-    return_kernel(*refs[:15], *[sems[i : i + 2] for i in range(0, 10, 2)])
+    sems = refs[17:]
+    return_kernel(*refs[:17], *[sems[i : i + 2] for i in range(0, 14, 2)])
 
 
 def fold_kernel(halo, centre_ref, row_hbm, side_hbm, corner_hbm, chunks_hbm, out_ref, probe_out, sides, middle, row_ref, side_ref, corner_ref, chunks_ref, probe_ref, load, extra, store):
@@ -665,7 +685,7 @@
     for p in range(2):
         for t in range(half_rows // 8):
             for h in range(n // LANE):
-                probe_ref[p, pl.ds(8 * t, 8), pl.ds(LANE * h, LANE)] = chunks_ref[at]
+                probe_ref[p, pl.ds(8 * t, 8), pl.ds(LANE * h, LANE)] = chunks_ref[at // 16, at // 4 % 4, at % 4]
                 at += 1
     stores[-1].start()
     for copy in stores:

time: 94 us -> 92.4 us (0.983)
  Pallas kernels: 92.7 us -> 91.5 us
    pallas_call x1, Pallas kernels: 33 us -> 31.9 us  [send_back(): pl.pallas_call(return_kernel_flat, out_shape=tuple((jax.ShapeDtypeStruct(...]
where the time goes in v5:
time: 92.4 us; the launch traced here: 92.2 us
  Pallas kernels  91.5 us (99%)
    pallas_call x1, Pallas kernels, exchange_halo(): pl.pallas_call(functools.partial(halo_kernel, half, halo), out_shape=(jax...  31.9 us
    pallas_call x1, Pallas kernels, send_back(): pl.pallas_call(return_kernel_flat, out_shape=tuple((jax.ShapeDtypeStruct(...  31.9 us
    pallas_call x1, Pallas kernels, waves(): pl.pallas_call(functools.partial(wave_kernel, half), out_shape=(jax.Shape...  13.9 us
    pallas_call x1, Pallas kernels, scatter(): pl.pallas_call(functools.partial(scatter_kernel, halo), out_shape=tuple((...  6.1 us
    pallas_call x1, Pallas kernels, extract(): pl.pallas_call(functools.partial(extract_kernel, n // 2), out_shape=(shap...  4.63 us
    pallas_call x1, Pallas kernels, fold(): pl.pallas_call(functools.partial(fold_kernel, halo), out_shape=(jax.Shape...  3.12 us

profile of v5, /device:TPU:0, one launch (start us, length us, event | category | flops | bytes accessed | tf_op | source)
XLA Modules:
  0.0 92.2 jit_solution(10011917591252027378)
XLA Ops:
  0.6 31.9 %halo_in.1 = (bf16[2,640,1280]{2,1,0:T(8,128)(2,1)}, f32[2,256,256]{2,1,0:T(8,128)}, f32[4,256,256]{2,1,0:T(8,128)}) custom-call(f32[256,256]{1,0:T(8,128)} %phases_ref.1, bf16[2,256,256]{2,1,0:T(8,128)(2,1)} %constant.5.clone.perm_ref, bf16[1,512,1024]{2,1,0:T(8,128)(2,1)} %re_ref.1, bf16[1,512,1024]{2,1,0:T(8,128)(2,1)} %im_ref.1, ...), custom_call_target="tpu_custom_call" | custom-call | tf_op jit(solution)/shard_map/halo_in/pallas_call | solution.py:222
  32.6 4.6 %extract.1 = (bf16[4,2,256,256]{3,2,1,0:T(8,128)(2,1)}, bf16[4,2,256,256]{3,2,1,0:T(8,128)(2,1)}) custom-call(s32[1,1,2,2,4]{4,3,2,1,0:T(2,128)} %bitcast.1, s32[1,1,4]{2,1,0:T(1,128)} %occupied.1, bf16[2,640,1280]{2,1,0:T(8,128)(2,1)} %get-tuple-element.18.pad_ref), custom_call_target="tpu_custom_call" | custom-call | tf_op jit(solution)/shard_map/extract/pallas_call | solution.py:296
  37.2 13.9 %waves.1 = (bf16[8,2,256,256]{3,2,1,0:T(8,128)(2,1)}, f32[2,256,256]{2,1,0:T(8,128)}) custom-call(f32[2,256,256]{2,1,0:T(8,128)} %probe_hbm.1, f32[2,256,256]{2,1,0:T(8,128)} %get-tuple-element.17.kern_hbm, bf16[8,256,256]{2,1,0:T(8,128)(2,1)} %constant.4.clone.mats_hbm, bf16[4,2,256,256]{3,2,1,0:T(8,128)(2,1)} %get-tuple-element.19.mine_ref, ...), custom_call_target="tpu_custom_call" | custom-call | tf_op jit(solution)/shard_map/waves/pallas_call | solution.py:414
  51.1 6.1 %scatter.1 = (f32[2,1,512,1024]{3,2,1,0:T(8,128)}, bf16[2,128,1024]{2,1,0:T(8,128)(2,1)}, bf16[2,2,512,128]{3,2,1,0:T(8,128)(2,1)}, bf16[2,2,128,128]{3,2,1,0:T(8,128)(2,1)}) custom-call(s32[1,1,2,2,4]{4,3,2,1,0:T(2,128)} %bitcast.2, bf16[8,2,256,256]{3,2,1,0:T(8,128)(2,1)} %get-tuple-element.22.terms_ref), custom_call_target="tpu_custom_call" | custom-call | tf_op jit(solution)/shard_map/scatter/pallas_call | solution.py:485
  57.2 31.9 %halo_out.1 = (bf16[2,128,1024]{2,1,0:T(8,128)(2,1)}, bf16[2,2,512,128]{3,2,1,0:T(8,128)(2,1)}, bf16[2,2,128,128]{3,2,1,0:T(8,128)(2,1)}, f32[4,4,4,8,128]{4,3,2,1,0:T(8,128)}) custom-call(bf16[2,128,1024]{2,1,0:T(8,128)(2,1)} %get-tuple-element.24.refs_0_, bf16[2,2,512,128]{3,2,1,0:T(8,128)(2,1)} %get-tuple-element.25.refs_1_, ...), custom_call_target="tpu_custom_call" | custom-call | tf_op jit(solution)/shard_map/halo_out/pallas_call | solution.py:622
  89.1 3.1 %fold.1 = (f32[2,1,512,1024]{3,2,1,0:T(8,128)}, f32[2,128,256]{2,1,0:T(8,128)}) custom-call(f32[2,1,512,1024]{3,2,1,0:T(8,128)} %get-tuple-element.23.centre_ref, bf16[2,128,1024]{2,1,0:T(8,128)(2,1)} %get-tuple-element.28.row_hbm, bf16[2,2,512,128]{3,2,1,0:T(8,128)(2,1)} %get-tuple-element.29.side_hbm, ...), custom_call_target="tpu_custom_call", output_to_operand_aliasing={{0}: (0, {})} | custom-call | tf_op jit(solution)/shard_map/fold/pallas_call | solution.py:698

commit v6 on v5

--- a/solution.py
+++ b/solution.py
@@ -278,7 +278,7 @@
             done[k, p] = jnp.where(live, window, 0.0).astype(BF16)
 
     for part, out in enumerate((theirs_ref, mine_ref)):
-        @pl.loop(0, half)
+        @pl.loop(0, half, unroll=2)
         def _(k):
             cut(part * half + k)
             pltpu.make_async_copy(done.at[part * half + k], out.at[k], store.at[part * half + k]).start()
@@ -458,7 +458,7 @@
     for p in range(2):
         acc[p] = jnp.zeros(acc.shape[1:], F32)
 
-        @pl.loop(0, count)
+        @pl.loop(0, count, unroll=8)
         def _(k):
             term_load(p, k).wait()
             row = centres[0, 0, lax.rem(k, slots), 0, k // slots] + halo * (r - 1)

time: 92.4 us -> 92.2 us (level)
  no operation moved by 1% of the time
where the time goes in v6:
time: 92.2 us; the launch traced here: 92 us
  Pallas kernels  91.3 us (99%)
    pallas_call x1, Pallas kernels, exchange_halo(): pl.pallas_call(functools.partial(halo_kernel, half, halo), out_shape=(jax...  31.9 us
    pallas_call x1, Pallas kernels, send_back(): pl.pallas_call(return_kernel_flat, out_shape=tuple((jax.ShapeDtypeStruct(...  31.9 us
    pallas_call x1, Pallas kernels, waves(): pl.pallas_call(functools.partial(wave_kernel, half), out_shape=(jax.Shape...  13.9 us
    pallas_call x1, Pallas kernels, scatter(): pl.pallas_call(functools.partial(scatter_kernel, halo), out_shape=tuple((...  5.93 us
    pallas_call x1, Pallas kernels, extract(): pl.pallas_call(functools.partial(extract_kernel, n // 2), out_shape=(shap...  4.59 us
    pallas_call x1, Pallas kernels, fold(): pl.pallas_call(functools.partial(fold_kernel, halo), out_shape=(jax.Shape...  3.12 us

profile of v6, /device:TPU:0, one launch (start us, length us, event | category | flops | bytes accessed | tf_op | source)
XLA Modules:
  0.0 92.0 jit_solution(9479193889525944856)
XLA Ops:
  0.6 31.9 %halo_in.1 = (bf16[2,640,1280]{2,1,0:T(8,128)(2,1)}, f32[2,256,256]{2,1,0:T(8,128)}, f32[4,256,256]{2,1,0:T(8,128)}) custom-call(f32[256,256]{1,0:T(8,128)} %phases_ref.1, bf16[2,256,256]{2,1,0:T(8,128)(2,1)} %constant.5.clone.perm_ref, bf16[1,512,1024]{2,1,0:T(8,128)(2,1)} %re_ref.1, bf16[1,512,1024]{2,1,0:T(8,128)(2,1)} %im_ref.1, ...), custom_call_target="tpu_custom_call" | custom-call | tf_op jit(solution)/shard_map/halo_in/pallas_call | solution.py:222
  32.6 4.6 %extract.1 = (bf16[4,2,256,256]{3,2,1,0:T(8,128)(2,1)}, bf16[4,2,256,256]{3,2,1,0:T(8,128)(2,1)}) custom-call(s32[1,1,2,2,4]{4,3,2,1,0:T(2,128)} %bitcast.1, s32[1,1,4]{2,1,0:T(1,128)} %occupied.1, bf16[2,640,1280]{2,1,0:T(8,128)(2,1)} %get-tuple-element.18.pad_ref), custom_call_target="tpu_custom_call" | custom-call | tf_op jit(solution)/shard_map/extract/pallas_call | solution.py:296
  37.1 13.9 %waves.1 = (bf16[8,2,256,256]{3,2,1,0:T(8,128)(2,1)}, f32[2,256,256]{2,1,0:T(8,128)}) custom-call(f32[2,256,256]{2,1,0:T(8,128)} %probe_hbm.1, f32[2,256,256]{2,1,0:T(8,128)} %get-tuple-element.17.kern_hbm, bf16[8,256,256]{2,1,0:T(8,128)(2,1)} %constant.4.clone.mats_hbm, bf16[4,2,256,256]{3,2,1,0:T(8,128)(2,1)} %get-tuple-element.19.mine_ref, ...), custom_call_target="tpu_custom_call" | custom-call | tf_op jit(solution)/shard_map/waves/pallas_call | solution.py:414
  51.1 5.9 %scatter.1 = (f32[2,1,512,1024]{3,2,1,0:T(8,128)}, bf16[2,128,1024]{2,1,0:T(8,128)(2,1)}, bf16[2,2,512,128]{3,2,1,0:T(8,128)(2,1)}, bf16[2,2,128,128]{3,2,1,0:T(8,128)(2,1)}) custom-call(s32[1,1,2,2,4]{4,3,2,1,0:T(2,128)} %bitcast.2, bf16[8,2,256,256]{3,2,1,0:T(8,128)(2,1)} %get-tuple-element.22.terms_ref), custom_call_target="tpu_custom_call" | custom-call | tf_op jit(solution)/shard_map/scatter/pallas_call | solution.py:485
  57.0 31.9 %halo_out.1 = (bf16[2,128,1024]{2,1,0:T(8,128)(2,1)}, bf16[2,2,512,128]{3,2,1,0:T(8,128)(2,1)}, bf16[2,2,128,128]{3,2,1,0:T(8,128)(2,1)}, f32[4,4,4,8,128]{4,3,2,1,0:T(8,128)}) custom-call(bf16[2,128,1024]{2,1,0:T(8,128)(2,1)} %get-tuple-element.24.refs_0_, bf16[2,2,512,128]{3,2,1,0:T(8,128)(2,1)} %get-tuple-element.25.refs_1_, ...), custom_call_target="tpu_custom_call" | custom-call | tf_op jit(solution)/shard_map/halo_out/pallas_call | solution.py:622
  88.9 3.1 %fold.1 = (f32[2,1,512,1024]{3,2,1,0:T(8,128)}, f32[2,128,256]{2,1,0:T(8,128)}) custom-call(f32[2,1,512,1024]{3,2,1,0:T(8,128)} %get-tuple-element.23.centre_ref, bf16[2,128,1024]{2,1,0:T(8,128)(2,1)} %get-tuple-element.28.row_hbm, bf16[2,2,512,128]{3,2,1,0:T(8,128)(2,1)} %get-tuple-element.29.side_hbm, ...), custom_call_target="tpu_custom_call", output_to_operand_aliasing={{0}: (0, {})} | custom-call | tf_op jit(solution)/shard_map/fold/pallas_call | solution.py:698
